TPU v7x, 256 devices: a whole 4x4x8 slice. The times are simulated.
256 devices in a mesh: dom: 32 (over y, z_lo, core), section: 8 (over x, z_hi).
Axes of the slice: x: 4, y: 4, z: 8 (z_hi: 2, z_lo: 4; z = z_hi * 4 + z_lo), core: 2. Of those that a mesh axis runs over, the one named last changes fastest.
Arguments:
- feats: bfloat16 [131072, 1024], P('dom', 'section'), may hold values from -6 to 6
- tile_vals: bfloat16 [8192, 128, 128], P('dom'), may hold values from -0.1875 to 0.1875
- src_slot: int32 [8192], P('dom'), may hold values from 0 to 95, as said below
- dst_tile: int32 [8192], P('dom'), may hold values from 0 to 31
- tile_count: int32 [32], P('dom'), may hold values from 128 to 256, as said below
- send_tile: int32 [32, 96], P('dom'), may hold values from 0 to 31
- w_fwd: bfloat16 [1024, 1024], replicated, may hold values from -0.1875 to 0.1875
- b_fwd: float32 [1024], replicated, may hold values from -3 to 3
- w_inv1: bfloat16 [1024, 1024], replicated, may hold values from -0.1875 to 0.1875
- b_inv1: float32 [1024], replicated, may hold values from -3 to 3
- w_inv2: bfloat16 [1024, 1024], replicated, may hold values from -0.1875 to 0.1875
- b_inv2: float32 [1024], replicated, may hold values from -3 to 3
- target: bfloat16 [131072, 1024], P(('dom', 'section')), may hold values from -2.5 to 2.5
Outputs:
- hidden: bfloat16 [131072, 1024], P(('dom', 'section'))
- target_prev: bfloat16 [131072, 1024], P(('dom', 'section'))
Inputs may be any that keep to these rules, and one draw needn't show every extreme that they name: `src_slot`: slots are numbered by sending partition, 3 each; in each partition's list the entry i names slot number pi(i mod 96) for a permutation pi of the partition. `tile_count`: some partition's list is full.
All inputs are finite; a program needn't handle non-finite values.
Results may differ from a plain program's by a relative error of at most 0.0042.
Values may be sent and summed in bfloat16 or wider, within the bound.
No kernel may reach another device: no remote copies, remote signals or barrier semaphores. Data moves between devices by JAX's collectives and lax.ppermute only.
A program may use at most 192 MiB of HBM per device.

v0:
```python
import jax
import jax.numpy as jnp
from jax import lax
from jax.sharding import PartitionSpec as P

BLOCK = 16


def per_device(
    feats,
    tile_vals,
    src_slot,
    dst_tile,
    tile_count,
    send_tile,
    w_fwd,
    b_fwd,
    w_inv1,
    b_inv1,
    w_inv2,
    b_inv2,
    target,
):
    node_rows, feat_cols = feats.shape
    tile_side = tile_vals.shape[1]
    row_tiles = node_rows // tile_side
    recv_count = send_tile.shape[1]
    flat_width = tile_side * feat_cols
    flat_blocks = feats.reshape(row_tiles, flat_width)
    tile_ids = jnp.arange(row_tiles, dtype=jnp.int32)
    pick_send = (send_tile[0][:, None] == tile_ids[None, :]).astype(jnp.bfloat16)
    outgoing = jnp.dot(pick_send, flat_blocks, preferred_element_type=jnp.float32).astype(
        jnp.bfloat16
    )
    received = lax.all_to_all(
        outgoing.reshape(recv_count, tile_side, feat_cols),
        "dom",
        split_axis=0,
        concat_axis=0,
        tiled=True,
    )
    received_flat = received.reshape(recv_count, flat_width)
    slot_ids = jnp.arange(recv_count, dtype=jnp.int32)
    live_count = tile_count[0]
    turns_needed = (live_count + BLOCK - 1) // BLOCK

    def accumulate(turn_index, running):
        offset = turn_index * BLOCK
        values_block = lax.dynamic_slice_in_dim(tile_vals, offset, BLOCK, 0)
        slot_block = lax.dynamic_slice_in_dim(src_slot, offset, BLOCK, 0)
        dest_block = lax.dynamic_slice_in_dim(dst_tile, offset, BLOCK, 0)
        pick_slot = (slot_block[:, None] == slot_ids[None, :]).astype(jnp.bfloat16)
        sources = jnp.dot(pick_slot, received_flat, preferred_element_type=jnp.float32).astype(
            jnp.bfloat16
        )
        products = jnp.einsum(
            "lab,lbc->lac",
            values_block,
            sources.reshape(BLOCK, tile_side, feat_cols),
            preferred_element_type=jnp.float32,
        )
        active = offset + jnp.arange(BLOCK, dtype=jnp.int32) < live_count
        place = ((tile_ids[:, None] == dest_block[None, :]) & active[None, :]).astype(jnp.float32)
        return running + jnp.dot(
            place, products.reshape(BLOCK, flat_width), precision=lax.Precision.HIGHEST
        )

    summed = lax.fori_loop(
        0, turns_needed, accumulate, jnp.zeros((row_tiles, flat_width), jnp.float32)
    )
    agg = summed.reshape(node_rows, feat_cols).astype(jnp.bfloat16)
    agg_rows, input_rows = (
        lax.all_to_all(agg, "section", split_axis=0, concat_axis=1, tiled=True),
        lax.all_to_all(feats, "section", split_axis=0, concat_axis=1, tiled=True),
    )
    hidden = jnp.tanh(jnp.dot(agg_rows, w_fwd, preferred_element_type=jnp.float32) + b_fwd).astype(
        jnp.bfloat16
    )

    def inverse(values):
        inner = jnp.tanh(
            jnp.dot(values, w_inv1, preferred_element_type=jnp.float32) + b_inv1
        ).astype(jnp.bfloat16)
        return jnp.tanh(jnp.dot(inner, w_inv2, preferred_element_type=jnp.float32) + b_inv2)

    shifted = input_rows.astype(jnp.float32) + inverse(target) - inverse(hidden)
    return (hidden, shifted.astype(jnp.bfloat16))


def solution(mesh):
    placed = (
        P("dom", "section"),
        P("dom", None, None),
        P("dom"),
        P("dom"),
        P("dom"),
        P("dom", None),
        P(),
        P(),
        P(),
        P(),
        P(),
        P(),
        P(("dom", "section"), None),
    )
    return jax.shard_map(
        per_device,
        mesh=mesh,
        in_specs=placed,
        out_specs=(P(("dom", "section"), None), P(("dom", "section"), None)),
        check_vma=False,
    )
```

profile of v0, /device:TPU:65, one launch (start us, length us, event | category | flops | bytes accessed | tf_op | source)
XLA Modules:
  0.0 304.0 jit_solution(7510623967146694801)
XLA Ops:
  5.9 8.7 %all-to-all-start = ((bf16[96,128,128]{2,1,0:T(8,128)(2,1)}), bf16[96,128,128]{2,1,0:T(8,128)(2,1)}, u32[]{:S(2)}, u32[]{:S(2)}) async-start(bf16[96,128,128]{2,1,0:T(8,128)(2,1)} %bitcast.56), calls=%async_computation | async-start | bytes 6291456 | tf_op jit(solution)/shard_map/all_to_all | solution.py:35
  15.2 68.0 %all-to-all-done = bf16[96,128,128]{2,1,0:T(8,128)(2,1)} async-done(((bf16[96,128,128]{2,1,0:T(8,128)(2,1)}), bf16[96,128,128]{2,1,0:T(8,128)(2,1)}, u32[]{:S(2)}, u32[]{:S(2)}) %all-to-all-start) | async-done | bytes 3145760 | tf_op jit(solution)/shard_map/all_to_all | solution.py:35
  83.2 6.0 %copy.32 = bf16[12,8,128,128]{3,1,2,0:T(8,128)(2,1)} copy(bf16[12,8,128,128]{3,2,1,0:T(8,128)(2,1)} %bitcast.14) | data formatting | bytes 6291456
  90.7 146.8 %while.11 = (s32[]{:T(128)}, f32[32,16384]{1,0:T(8,128)}, s32[]{:T(128)}, s32[256]{0:T(256)S(1)}, s32[]{:T(128)}, /*index=5*/bf16[256,128,128]{2,1,0:T(8,128)(2,...) while((s32[]{:T(128)}, f32[32,16384]{1,0:T(8,128)}, ...), condition=%wide.region_1.2_spmd.clone, body=%wide.region_0.1_spmd.clone.sunk | while | flops 218892832 | bytes 12059223 | solution.py:68
  95.4 4.5 %convolution_add_fusion.2 = f32[32,16384]{1,0:T(8,128)} fusion(f32[32,16384]{1,0:T(8,128)} %get-tuple-element.155, f32[2,8,128,128]{3,2,1,0:T(8,128)S(1)} %bitcast.54, s32[16]{0:T(128)S(1)} %dynamic_slice.19, pred[16]{0:T(512)(128)(4,1)S(1)} %add_compare_fusion.2), kind=kOutput, calls=%fused_computation.2.clone.1 | convolution fusion | flops 101188608 | bytes 5242960 | tf_op jit(solution)/shard_map/while/body/dot_general | solution.py:64
  104.6 4.5 %convolution_add_fusion.2 = f32[32,16384]{1,0:T(8,128)} fusion(f32[32,16384]{1,0:T(8,128)} %get-tuple-element.155, f32[2,8,128,128]{3,2,1,0:T(8,128)S(1)} %bitcast.54, s32[16]{0:T(128)S(1)} %dynamic_slice.19, pred[16]{0:T(512)(128)(4,1)S(1)} %add_compare_fusion.2), kind=kOutput, calls=%fused_computation.2.clone.1 | convolution fusion | flops 101188608 | bytes 5242960 | tf_op jit(solution)/shard_map/while/body/dot_general | solution.py:64
  113.8 4.5 %convolution_add_fusion.2 = f32[32,16384]{1,0:T(8,128)} fusion(f32[32,16384]{1,0:T(8,128)} %get-tuple-element.155, f32[2,8,128,128]{3,2,1,0:T(8,128)S(1)} %bitcast.54, s32[16]{0:T(128)S(1)} %dynamic_slice.19, pred[16]{0:T(512)(128)(4,1)S(1)} %add_compare_fusion.2), kind=kOutput, calls=%fused_computation.2.clone.1 | convolution fusion | flops 101188608 | bytes 5242960 | tf_op jit(solution)/shard_map/while/body/dot_general | solution.py:64
  122.9 4.4 %convolution_add_fusion.2 = f32[32,16384]{1,0:T(8,128)} fusion(f32[32,16384]{1,0:T(8,128)} %get-tuple-element.155, f32[2,8,128,128]{3,2,1,0:T(8,128)S(1)} %bitcast.54, s32[16]{0:T(128)S(1)} %dynamic_slice.19, pred[16]{0:T(512)(128)(4,1)S(1)} %add_compare_fusion.2), kind=kOutput, calls=%fused_computation.2.clone.1 | convolution fusion | flops 101188608 | bytes 5242960 | tf_op jit(solution)/shard_map/while/body/dot_general | solution.py:64
  132.1 4.5 %convolution_add_fusion.2 = f32[32,16384]{1,0:T(8,128)} fusion(f32[32,16384]{1,0:T(8,128)} %get-tuple-element.155, f32[2,8,128,128]{3,2,1,0:T(8,128)S(1)} %bitcast.54, s32[16]{0:T(128)S(1)} %dynamic_slice.19, pred[16]{0:T(512)(128)(4,1)S(1)} %add_compare_fusion.2), kind=kOutput, calls=%fused_computation.2.clone.1 | convolution fusion | flops 101188608 | bytes 5242960 | tf_op jit(solution)/shard_map/while/body/dot_general | solution.py:64
  141.3 4.5 %convolution_add_fusion.2 = f32[32,16384]{1,0:T(8,128)} fusion(f32[32,16384]{1,0:T(8,128)} %get-tuple-element.155, f32[2,8,128,128]{3,2,1,0:T(8,128)S(1)} %bitcast.54, s32[16]{0:T(128)S(1)} %dynamic_slice.19, pred[16]{0:T(512)(128)(4,1)S(1)} %add_compare_fusion.2), kind=kOutput, calls=%fused_computation.2.clone.1 | convolution fusion | flops 101188608 | bytes 5242960 | tf_op jit(solution)/shard_map/while/body/dot_general | solution.py:64
  150.5 4.4 %convolution_add_fusion.2 = f32[32,16384]{1,0:T(8,128)} fusion(f32[32,16384]{1,0:T(8,128)} %get-tuple-element.155, f32[2,8,128,128]{3,2,1,0:T(8,128)S(1)} %bitcast.54, s32[16]{0:T(128)S(1)} %dynamic_slice.19, pred[16]{0:T(512)(128)(4,1)S(1)} %add_compare_fusion.2), kind=kOutput, calls=%fused_computation.2.clone.1 | convolution fusion | flops 101188608 | bytes 5242960 | tf_op jit(solution)/shard_map/while/body/dot_general | solution.py:64
  159.6 4.5 %convolution_add_fusion.2 = f32[32,16384]{1,0:T(8,128)} fusion(f32[32,16384]{1,0:T(8,128)} %get-tuple-element.155, f32[2,8,128,128]{3,2,1,0:T(8,128)S(1)} %bitcast.54, s32[16]{0:T(128)S(1)} %dynamic_slice.19, pred[16]{0:T(512)(128)(4,1)S(1)} %add_compare_fusion.2), kind=kOutput, calls=%fused_computation.2.clone.1 | convolution fusion | flops 101188608 | bytes 5242960 | tf_op jit(solution)/shard_map/while/body/dot_general | solution.py:64
  168.8 4.5 %convolution_add_fusion.2 = f32[32,16384]{1,0:T(8,128)} fusion(f32[32,16384]{1,0:T(8,128)} %get-tuple-element.155, f32[2,8,128,128]{3,2,1,0:T(8,128)S(1)} %bitcast.54, s32[16]{0:T(128)S(1)} %dynamic_slice.19, pred[16]{0:T(512)(128)(4,1)S(1)} %add_compare_fusion.2), kind=kOutput, calls=%fused_computation.2.clone.1 | convolution fusion | flops 101188608 | bytes 5242960 | tf_op jit(solution)/shard_map/while/body/dot_general | solution.py:64
  178.0 4.4 %convolution_add_fusion.2 = f32[32,16384]{1,0:T(8,128)} fusion(f32[32,16384]{1,0:T(8,128)} %get-tuple-element.155, f32[2,8,128,128]{3,2,1,0:T(8,128)S(1)} %bitcast.54, s32[16]{0:T(128)S(1)} %dynamic_slice.19, pred[16]{0:T(512)(128)(4,1)S(1)} %add_compare_fusion.2), kind=kOutput, calls=%fused_computation.2.clone.1 | convolution fusion | flops 101188608 | bytes 5242960 | tf_op jit(solution)/shard_map/while/body/dot_general | solution.py:64
  187.2 4.5 %convolution_add_fusion.2 = f32[32,16384]{1,0:T(8,128)} fusion(f32[32,16384]{1,0:T(8,128)} %get-tuple-element.155, f32[2,8,128,128]{3,2,1,0:T(8,128)S(1)} %bitcast.54, s32[16]{0:T(128)S(1)} %dynamic_slice.19, pred[16]{0:T(512)(128)(4,1)S(1)} %add_compare_fusion.2), kind=kOutput, calls=%fused_computation.2.clone.1 | convolution fusion | flops 101188608 | bytes 5242960 | tf_op jit(solution)/shard_map/while/body/dot_general | solution.py:64
  196.3 4.5 %convolution_add_fusion.2 = f32[32,16384]{1,0:T(8,128)} fusion(f32[32,16384]{1,0:T(8,128)} %get-tuple-element.155, f32[2,8,128,128]{3,2,1,0:T(8,128)S(1)} %bitcast.54, s32[16]{0:T(128)S(1)} %dynamic_slice.19, pred[16]{0:T(512)(128)(4,1)S(1)} %add_compare_fusion.2), kind=kOutput, calls=%fused_computation.2.clone.1 | convolution fusion | flops 101188608 | bytes 5242960 | tf_op jit(solution)/shard_map/while/body/dot_general | solution.py:64
  205.5 4.4 %convolution_add_fusion.2 = f32[32,16384]{1,0:T(8,128)} fusion(f32[32,16384]{1,0:T(8,128)} %get-tuple-element.155, f32[2,8,128,128]{3,2,1,0:T(8,128)S(1)} %bitcast.54, s32[16]{0:T(128)S(1)} %dynamic_slice.19, pred[16]{0:T(512)(128)(4,1)S(1)} %add_compare_fusion.2), kind=kOutput, calls=%fused_computation.2.clone.1 | convolution fusion | flops 101188608 | bytes 5242960 | tf_op jit(solution)/shard_map/while/body/dot_general | solution.py:64
  214.7 4.5 %convolution_add_fusion.2 = f32[32,16384]{1,0:T(8,128)} fusion(f32[32,16384]{1,0:T(8,128)} %get-tuple-element.155, f32[2,8,128,128]{3,2,1,0:T(8,128)S(1)} %bitcast.54, s32[16]{0:T(128)S(1)} %dynamic_slice.19, pred[16]{0:T(512)(128)(4,1)S(1)} %add_compare_fusion.2), kind=kOutput, calls=%fused_computation.2.clone.1 | convolution fusion | flops 101188608 | bytes 5242960 | tf_op jit(solution)/shard_map/while/body/dot_general | solution.py:64
  223.9 4.5 %convolution_add_fusion.2 = f32[32,16384]{1,0:T(8,128)} fusion(f32[32,16384]{1,0:T(8,128)} %get-tuple-element.155, f32[2,8,128,128]{3,2,1,0:T(8,128)S(1)} %bitcast.54, s32[16]{0:T(128)S(1)} %dynamic_slice.19, pred[16]{0:T(512)(128)(4,1)S(1)} %add_compare_fusion.2), kind=kOutput, calls=%fused_computation.2.clone.1 | convolution fusion | flops 101188608 | bytes 5242960 | tf_op jit(solution)/shard_map/while/body/dot_general | solution.py:64
  233.0 4.4 %convolution_add_fusion.2 = f32[32,16384]{1,0:T(8,128)} fusion(f32[32,16384]{1,0:T(8,128)} %get-tuple-element.155, f32[2,8,128,128]{3,2,1,0:T(8,128)S(1)} %bitcast.54, s32[16]{0:T(128)S(1)} %dynamic_slice.19, pred[16]{0:T(512)(128)(4,1)S(1)} %add_compare_fusion.2), kind=kOutput, calls=%fused_computation.2.clone.1 | convolution fusion | flops 101188608 | bytes 5242960 | tf_op jit(solution)/shard_map/while/body/dot_general | solution.py:64
  240.5 29.7 %all_to_all.34 = bf16[8,512,128]{2,1,0:T(8,128)(2,1)S(1)} all-to-all(bf16[8,512,128]{2,1,0:T(8,128)(2,1)} %convert_element_type.39), channel_id=1, replica_groups=mesh['dom'=32,'section'=8] {'section'}, dimensions={0} | all-to-all | bytes 2097152 | tf_op jit(solution)/shard_map/all_to_all | solution.py:73
  274.7 5.6 %fusion.18 = f32[512,1024]{1,0:T(8,128)} fusion(bf16[1024,1024]{1,0:T(8,128)(2,1)S(1)} %copy-done, bf16[512,1024]{1,0:T(8,128)(2,1)} %param.27, bf16[1024,1024]{1,0:T(8,128)(2,1)} %param.23, f32[1024]{0:T(1024)S(1)} %copy-done.3), kind=kOutput, calls=%fused_computation.27 | convolution fusion | flops 2148532224 | bytes 7344128 | tf_op jit(solution)/shard_map/dot_general | solution.py:84
  285.8 11.9 %all-to-all-done.2 = bf16[8,512,128]{2,1,0:T(8,128)(2,1)} async-done(((bf16[8,512,128]{2,1,0:T(8,128)(2,1)}), bf16[8,512,128]{2,1,0:T(8,128)(2,1)}, u32[]{:S(2)}, u32[]{:S(2)}) %all-to-all-start.2) | async-done | bytes 1048608 | tf_op jit(solution)/shard_map/all_to_all | solution.py:74
  297.7 6.3 %fusion.16 = bf16[512,1024]{1,0:T(8,128)(2,1)} fusion(f32[512,1024]{1,0:T(8,128)} %fusion.18, bf16[1024,1024]{1,0:T(8,128)(2,1)S(1)} %copy-done, f32[1024]{0:T(1024)S(1)} %copy-done.4, bf16[512,1024]{1,0:T(8,128)(2,1)} %tanh_convert_fusion.2, bf16[1024,1024]{1,0:T(8,128)(2,1)} %param.23, f32[1024]{0:T(1024)S(1)} %copy-done.3, ...), kind=kOutput, calls=%fused_computation.21 | convolution fusion | flops 2151677952 | bytes 9445376 | tf_op jit(solution)/shard_map/dot_general | solution.py:84
  (119 shorter events, 94.9 us)
Async XLA Ops:
  0.6 274.1 %copy-start = (bf16[1024,1024]{1,0:T(8,128)(2,1)S(1)}, bf16[1024,1024]{1,0:T(8,128)(2,1)}, u32[]{:S(2)}) copy-start(bf16[1024,1024]{1,0:T(8,128)(2,1)} %param.25) | copy-start | bytes 6291460
  0.6 1.7 copy-start.1
  5.9 77.3 %all-to-all-start = ((bf16[96,128,128]{2,1,0:T(8,128)(2,1)}), bf16[96,128,128]{2,1,0:T(8,128)(2,1)}, u32[]{:S(2)}, u32[]{:S(2)}) async-start(bf16[96,128,128]{2,1,0:T(8,128)(2,1)} %bitcast.56), calls=%async_computation | async-start | bytes 6291456 | tf_op jit(solution)/shard_map/all_to_all | solution.py:35
  89.2 1.5 copy-start.5
  89.2 1.5 copy-start.6
  240.5 34.2 %copy-start.3 = (f32[1024]{0:T(1024)S(1)}, f32[1024]{0:T(1024)}, u32[]{:S(2)}) copy-start(f32[1024]{0:T(1024)} %param.24) | copy-start | bytes 12292
  270.3 27.5 %all-to-all-start.2 = ((bf16[8,512,128]{2,1,0:T(8,128)(2,1)}), bf16[8,512,128]{2,1,0:T(8,128)(2,1)}, u32[]{:S(2)}, u32[]{:S(2)}) async-start(bf16[8,512,128]{2,1,0:T(8,128)(2,1)} %bitcast.4), calls=%async_computation.2 | async-start | bytes 2097152 | tf_op jit(solution)/shard_map/all_to_all | solution.py:74
  280.3 1.3 copy-start.2
  281.6 16.1 %copy-start.4 = (f32[1024]{0:T(1024)S(1)}, f32[1024]{0:T(1024)}, u32[]{:S(2)}) copy-start(f32[1024]{0:T(1024)} %param.26) | copy-start | bytes 12292
where the time goes:
time: 306 us; the launch traced here: 304 us
  matrix products  149 us (49%)
  waiting for transfers between devices  79.9 us (26%)
  blocking collectives  29.7 us (10%)
  local copies, waits for them, and re-layouts  18.4 us (6%)
  starting transfers between devices  13.1 us (4%)
  other arithmetic  12.1 us (4%)
    dot_general x16, matrix products, accumulate(): jnp.dot(place, products.reshape(BLOCK, flat_width), precision=lax.Precisi...  71.2 us
    all_to_all x1, waiting for transfers between devices, per_device(): lax.all_to_all(outgoing.reshape(recv_count, tile_side, feat_cols), 'dom',...  68 us
    dot_general x16, matrix products, accumulate(): jnp.dot(pick_slot, received_flat, preferred_element_type=jnp.float32)  39.4 us
    all_to_all x1, blocking collectives, per_device(): lax.all_to_all(agg, 'section', split_axis=0, concat_axis=1, tiled=True)  29.7 us
    dot_general x16, matrix products, accumulate(): jnp.einsum('lab,lbc->lac', values_block, sources.reshape(BLOCK, tile_side...  21.4 us
    all_to_all x1, waiting for transfers between devices, per_device(): lax.all_to_all(feats, 'section', split_axis=0, concat_axis=1, tiled=True)  11.9 us
    dot_general x2, matrix products, inverse(): jnp.dot(inner, w_inv2, preferred_element_type=jnp.float32) + b_inv2  11.8 us
    lt x16, other arithmetic, accumulate(): active = offset + jnp.arange(BLOCK, dtype=jnp.int32) < live_count  10.4 us
  transfers between devices with their start and end apart: 2, of which 2 were waited for; matrix products, arithmetic and copies ran while one was open for 4% of the time, Pallas kernels for 0%

commit v1 on v0

v1 whole, which is shorter than its diff:
```python
import jax
import jax.numpy as jnp
from jax import lax
from jax.experimental import pallas as pl
from jax.experimental.pallas import tpu as pltpu
from jax.sharding import PartitionSpec as P

CHUNK = 16
UNROLL = 4


def pack_tiles(feats, send_ids):
    row_tiles, side, cols = feats.shape
    slots = send_ids.shape[0]

    def body(ids, src, out, sem):
        def issue(i, _):
            pltpu.make_async_copy(src.at[ids[i]], out.at[i], sem).start()
            return 0

        lax.fori_loop(0, slots, issue, 0, unroll=8)
        pltpu.make_async_copy(out, out, sem).wait()

    return pl.pallas_call(
        body,
        grid_spec=pltpu.PrefetchScalarGridSpec(
            num_scalar_prefetch=1,
            grid=(1,),
            in_specs=[pl.BlockSpec((row_tiles, side, cols), lambda i, ids: (0, 0, 0))],
            out_specs=pl.BlockSpec(memory_space=pl.ANY),
            scratch_shapes=[pltpu.SemaphoreType.DMA],
        ),
        out_shape=jax.ShapeDtypeStruct((slots, side, cols), feats.dtype),
        name="pack_tiles",
    )(send_ids, feats)


def aggregate(received, tile_vals, src_slot, dst_tile, tile_count, row_tiles):
    slots, side, cols = received.shape
    entries = tile_vals.shape[0]
    levels = pl.cdiv(entries, slots)
    tail = entries - (levels - 1) * slots
    chunks = slots // CHUNK

    def copies(vals, store, sems, chunk):
        base = chunk * CHUNK
        out = []
        for level in range(levels):
            if level == levels - 1 and base >= tail:
                continue
            out.append(
                pltpu.make_async_copy(
                    vals.at[pl.ds(level * slots + base, CHUNK)],
                    store.at[pl.ds(base, CHUNK), level],
                    sems.at[chunk, level],
                )
            )
        return out

    def body(slot_ref, dst_ref, count_ref, recv, vals, out, store, acc, sems):
        for chunk in range(chunks):
            for copy in copies(vals, store, sems, chunk):
                copy.start()
        acc[...] = jnp.zeros_like(acc)
        count = count_ref[0]
        for chunk in range(chunks):
            waits = copies(vals, store, sems, chunk)
            for copy in waits:
                copy.wait()
            live_levels = len(waits)

            def step(turn, _):
                for k in range(UNROLL):
                    j = chunk * CHUNK + turn * UNROLL + k
                    source = recv[slot_ref[j]]
                    left = store[j, :live_levels].reshape(live_levels * side, side)
                    product = jnp.dot(left, source, preferred_element_type=jnp.float32)
                    for level in range(live_levels):
                        i = j + level * slots
                        place = jnp.where(i < count, dst_ref[i], row_tiles)
                        acc[place] += product[level * side : (level + 1) * side]
                return 0

            lax.fori_loop(0, CHUNK // UNROLL, step, 0)
        for tile in range(row_tiles):
            out[tile] = acc[tile].astype(out.dtype)

    return pl.pallas_call(
        body,
        grid_spec=pltpu.PrefetchScalarGridSpec(
            num_scalar_prefetch=3,
            grid=(1,),
            in_specs=[
                pl.BlockSpec((slots, side, cols), lambda i, *_: (0, 0, 0)),
                pl.BlockSpec(memory_space=pl.ANY),
            ],
            out_specs=pl.BlockSpec((row_tiles, side, cols), lambda i, *_: (0, 0, 0)),
            scratch_shapes=[
                pltpu.VMEM((slots, levels, side, side), tile_vals.dtype),
                pltpu.VMEM((row_tiles + 1, side, cols), jnp.float32),
                pltpu.SemaphoreType.DMA((chunks, levels)),
            ],
        ),
        out_shape=jax.ShapeDtypeStruct((row_tiles, side, cols), received.dtype),
        compiler_params=pltpu.CompilerParams(vmem_limit_bytes=32 << 20),
        cost_estimate=pl.CostEstimate(
            flops=2 * entries * side * side * cols,
            bytes_accessed=entries * side * side * 2 + (slots + row_tiles) * side * cols * 2,
            transcendentals=0,
        ),
        name="aggregate",
    )(src_slot, dst_tile, tile_count, received, tile_vals)


def finish(agg, inputs, g_target, w_fwd, b_fwd, w_inv1, b_inv1, w_inv2, b_inv2):
    groups, rows, cols = agg.shape
    width = groups * cols
    block = 256

    def body(agg_ref, in_ref, gt_ref, wf, bf, w1, b1, w2, b2, hid_ref, out_ref):
        rows_in = jnp.concatenate([agg_ref[g] for g in range(groups)], axis=1)
        hidden = jnp.tanh(jnp.dot(rows_in, wf[...], preferred_element_type=jnp.float32) + bf[...])
        hidden = hidden.astype(hid_ref.dtype)
        hid_ref[...] = hidden
        inner = jnp.tanh(jnp.dot(hidden, w1[...], preferred_element_type=jnp.float32) + b1[...])
        inner = inner.astype(hid_ref.dtype)
        back = jnp.tanh(jnp.dot(inner, w2[...], preferred_element_type=jnp.float32) + b2[...])
        feats = jnp.concatenate([in_ref[g] for g in range(groups)], axis=1).astype(jnp.float32)
        out_ref[...] = (feats + gt_ref[...] - back).astype(out_ref.dtype)

    split = pl.BlockSpec((groups, block, cols), lambda i: (0, i, 0))
    whole = pl.BlockSpec((block, width), lambda i: (i, 0))
    weight = pl.BlockSpec((width, width), lambda i: (0, 0))
    bias = pl.BlockSpec((1, width), lambda i: (0, 0))
    return pl.pallas_call(
        body,
        grid=(rows // block,),
        in_specs=[split, split, whole, weight, bias, weight, bias, weight, bias],
        out_specs=[whole, whole],
        out_shape=[jax.ShapeDtypeStruct((rows, width), agg.dtype)] * 2,
        compiler_params=pltpu.CompilerParams(vmem_limit_bytes=40 << 20),
        cost_estimate=pl.CostEstimate(
            flops=6 * rows * width * width,
            bytes_accessed=6 * width * width + 12 * rows * width,
            transcendentals=3 * rows * width,
        ),
        name="finish",
    )(agg, inputs, g_target, w_fwd, b_fwd[None], w_inv1, b_inv1[None], w_inv2, b_inv2[None])


def per_device(
    feats,
    tile_vals,
    src_slot,
    dst_tile,
    tile_count,
    send_tile,
    w_fwd,
    b_fwd,
    w_inv1,
    b_inv1,
    w_inv2,
    b_inv2,
    target,
):
    node_rows, feat_cols = feats.shape
    side = tile_vals.shape[1]
    row_tiles = node_rows // side
    rows = target.shape[0]
    groups = node_rows // rows
    outgoing = pack_tiles(feats.reshape(row_tiles, side, feat_cols), send_tile[0])
    received = lax.all_to_all(outgoing, "dom", split_axis=0, concat_axis=0, tiled=True)
    inner = jnp.tanh(jnp.dot(target, w_inv1, preferred_element_type=jnp.float32) + b_inv1).astype(
        jnp.bfloat16
    )
    g_target = jnp.tanh(jnp.dot(inner, w_inv2, preferred_element_type=jnp.float32) + b_inv2)
    received, g_target = lax.optimization_barrier((received, g_target))
    agg = aggregate(received, tile_vals, src_slot, dst_tile, tile_count, row_tiles)
    agg_rows = lax.all_to_all(
        agg.reshape(groups, rows, feat_cols), "section", split_axis=0, concat_axis=0, tiled=True
    )
    input_rows = lax.all_to_all(
        feats.reshape(groups, rows, feat_cols), "section", split_axis=0, concat_axis=0, tiled=True
    )
    hidden, shifted = finish(
        agg_rows, input_rows, g_target, w_fwd, b_fwd, w_inv1, b_inv1, w_inv2, b_inv2
    )
    return (hidden, shifted)


def solution(mesh):
    placed = (
        P("dom", "section"),
        P("dom", None, None),
        P("dom"),
        P("dom"),
        P("dom"),
        P("dom", None),
        P(),
        P(),
        P(),
        P(),
        P(),
        P(),
        P(("dom", "section"), None),
    )
    return jax.shard_map(
        per_device,
        mesh=mesh,
        in_specs=placed,
        out_specs=(P(("dom", "section"), None), P(("dom", "section"), None)),
        check_vma=False,
    )
```

time: 306 us -> 164 us (0.54)
  the two profiles are of different devices: /device:TPU:65 before, /device:TPU:24 now
where the time goes in v1:
time: 164 us
  blocking collectives  112 us (68%)
  Pallas kernels  16.1 us (10%)
  local copies, waits for them, and re-layouts  10.1 us (6%)
  waiting for transfers between devices  10 us (6%)
  starting transfers between devices  8.36 us (5%)
  matrix products  5.94 us (4%)
    all_to_all x1, blocking collectives, per_device(): lax.all_to_all(outgoing, 'dom', split_axis=0, concat_axis=0, tiled=True)  79.7 us
    all_to_all x1, blocking collectives, per_device(): lax.all_to_all(agg.reshape(groups, rows, feat_cols), 'section', split_axi...  31.9 us
    unnamed x24, local copies, waits for them, and re-layouts  10.1 us
    all_to_all x1, waiting for transfers between devices, per_device(): lax.all_to_all(feats.reshape(groups, rows, feat_cols), 'section', split_a...  10 us
    all_to_all x1, starting transfers between devices, per_device(): lax.all_to_all(feats.reshape(groups, rows, feat_cols), 'section', split_a...  8.36 us
    pallas_call x1, Pallas kernels, aggregate(): pl.pallas_call(body, grid_spec=pltpu.PrefetchScalarGridSpec(num_scalar_pr...  7.8 us
    dot_general x1, matrix products, per_device(): jnp.dot(inner, w_inv2, preferred_element_type=jnp.float32) + b_inv2  5.94 us
    pallas_call x1, Pallas kernels, finish(): pl.pallas_call(body, grid=(rows // block,), in_specs=[split, split, whole...  4.65 us
  transfers between devices with their start and end apart: 1, of which 1 were waited for; matrix products, arithmetic and copies ran while one was open for 4% of the time, Pallas kernels for 5%

profile of v1, /device:TPU:24, one launch (start us, length us, event | category | flops | bytes accessed | tf_op | source)
XLA Modules:
  0.0 163.5 jit_solution(978218907812678394)
XLA Ops:
  0.6 0.0 copy-start
  0.6 3.7 %pack_tiles.1 = bf16[96,128,128]{2,1,0:T(8,128)(2,1)} custom-call(s32[96]{0:T(128)} %bitcast.14, bf16[32,128,128]{2,1,0:T(8,128)(2,1)} %bitcast.1.src), custom_call_target="tpu_custom_call" | custom-call | tf_op jit(solution)/shard_map/pack_tiles/pallas_call | solution.py:24
  4.3 79.7 %all_to_all.15.recv = bf16[96,128,128]{2,1,0:T(8,128)(2,1)} all-to-all(bf16[96,128,128]{2,1,0:T(8,128)(2,1)} %pack_tiles.1), channel_id=1, replica_groups=mesh['dom'=32,'section'=8] {'dom'}, dimensions={0} | all-to-all | bytes 6291456 | tf_op jit(solution)/shard_map/all_to_all | solution.py:172
  84.1 8.4 %all-to-all-start.2 = ((bf16[8,512,128]{2,1,0:T(8,128)(2,1)}), bf16[8,512,128]{2,1,0:T(8,128)(2,1)S(1)}, u32[]{:S(2)}, u32[]{:S(2)}) async-start(bf16[8,512,128]{2,1,0:T(8,128)(2,1)} %bitcast.3), calls=%async_computation.2 | async-start | bytes 2097152 | tf_op jit(solution)/shard_map/all_to_all | solution.py:182
  93.1 0.0 copy-done
  93.1 0.0 copy-done.8
  93.1 0.0 copy-done.9
  93.1 0.0 copy-start.3
  93.1 0.0 copy-start.4
  93.1 5.9 %add_tanh_fusion.gt_ref = f32[512,1024]{1,0:T(8,128)} fusion(bf16[1024,1024]{1,0:T(8,128)(2,1)} %w2.1, f32[1024]{0:T(1024)S(1)} %copy-done.8, bf16[512,1024]{1,0:T(8,128)(2,1)S(1)} %copy-done, bf16[1024,1024]{1,0:T(8,128)(2,1)} %w1.1, f32[1024]{0:T(1024)S(1)} %copy-done.9), kind=kOutput, calls=%fused_computation | convolution fusion | flops 2149056512 | bytes 7348224 | tf_op jit(solution)/shard_map/dot_general | solution.py:176
  99.1 0.0 copy-done.3
  99.1 0.0 copy-done.4
  99.1 1.9 %copy-done.1 = bf16[96,128,128]{2,1,0:T(8,128)(2,1)S(1)} copy-done((bf16[96,128,128]{2,1,0:T(8,128)(2,1)S(1)}, bf16[96,128,128]{2,1,0:T(8,128)(2,1)}, u32[]{:S(2)}) %copy-start.1) | copy-done | bytes 3145752
  101.0 3.4 %copy-done.2 = bf16[256,128,128]{2,1,0:T(8,128)(2,1)S(1)} copy-done((bf16[256,128,128]{2,1,0:T(8,128)(2,1)S(1)}, bf16[256,128,128]{2,1,0:T(8,128)(2,1)}, u32[]{:S(2)}) %copy-start.2) | copy-done | bytes 8388632
  104.4 7.8 %aggregate.1 = bf16[32,128,128]{2,1,0:T(8,128)(2,1)S(1)} custom-call(s32[256]{0:T(256)S(1)} %copy-done.3, s32[256]{0:T(256)S(1)} %copy-done.4, s32[1]{0:T(128)S(6)} %copy.15.count_ref, bf16[96,128,128]{2,1,0:T(8,128)(2,1)S(1)} %copy-done.1, bf16[256,128,128]{2,1,0:T(8,128)(2,1)S(1)} %copy-done.2), custom_call_target="tpu_custom_call" | custom-call | flops 1073741824 | bytes 12582912 | tf_op jit(solution)/shard_map/aggregate/pallas_call | solution.py:88
  112.2 0.0 copy-start.10
  112.2 10.0 %all-to-all-done.2.in_ref = bf16[8,512,128]{2,1,0:T(8,128)(2,1)S(1)} async-done(((bf16[8,512,128]{2,1,0:T(8,128)(2,1)}), bf16[8,512,128]{2,1,0:T(8,128)(2,1)S(1)}, u32[]{:S(2)}, u32[]{:S(2)}) %all-to-all-start.2) | async-done | bytes 1048608 | tf_op jit(solution)/shard_map/all_to_all | solution.py:182
  122.2 31.9 %all_to_all.16.agg_ref = bf16[8,512,128]{2,1,0:T(8,128)(2,1)S(1)} all-to-all(bf16[8,512,128]{2,1,0:T(8,128)(2,1)S(1)} %bitcast.10), channel_id=1, replica_groups=mesh['dom'=32,'section'=8] {'section'}, dimensions={0} | all-to-all | bytes 2097152 | tf_op jit(solution)/shard_map/all_to_all | solution.py:179
  154.1 0.0 copy-done.10
  154.1 0.0 copy-done.5
  154.1 1.6 copy-done.6
  155.7 1.6 copy-done.7
  157.3 1.6 copy-done.11
  158.9 4.6 %finish.1 = (bf16[512,1024]{1,0:T(8,128)(2,1)}, bf16[512,1024]{1,0:T(8,128)(2,1)}) custom-call(bf16[8,512,128]{2,1,0:T(8,128)(2,1)S(1)} %all_to_all.16.agg_ref, bf16[8,512,128]{2,1,0:T(8,128)(2,1)S(1)} %all-to-all-done.2.in_ref, f32[512,1024]{1,0:T(8,128)S(1)} %copy-done.11, bf16[1024,1024]{1,0:T(8,128)(2,1)S(1)} %copy-done.7, f32[1,1024]{1,0:T(1,128)S(1)} %bitcast.13, ...), custom_call_target="tpu_custom_call" | custom-call | flops 3221225472 | bytes 12582912 | tf_op jit(solution)/shard_map/finish/pallas_call | solution.py:135
  (8 shorter events, 0.0 us)
Async XLA Ops:
  0.6 92.5 %copy-start = (bf16[512,1024]{1,0:T(8,128)(2,1)S(1)}, bf16[512,1024]{1,0:T(8,128)(2,1)}, u32[]{:S(2)}) copy-start(bf16[512,1024]{1,0:T(8,128)(2,1)} %param.25) | copy-start | bytes 3145732
  84.1 9.0 %copy-start.8 = (f32[1024]{0:T(1024)S(1)}, f32[1024]{0:T(1024)}, u32[]{:S(2)}) copy-start(f32[1024]{0:T(1024)} %param.24) | copy-start | bytes 12292
  84.1 9.0 %copy-start.9 = (f32[1024]{0:T(1024)S(1)}, f32[1024]{0:T(1024)}, u32[]{:S(2)}) copy-start(f32[1024]{0:T(1024)} %param.22) | copy-start | bytes 12292
  84.1 38.1 %all-to-all-start.2 = ((bf16[8,512,128]{2,1,0:T(8,128)(2,1)}), bf16[8,512,128]{2,1,0:T(8,128)(2,1)S(1)}, u32[]{:S(2)}, u32[]{:S(2)}) async-start(bf16[8,512,128]{2,1,0:T(8,128)(2,1)} %bitcast.3), calls=%async_computation.2 | async-start | bytes 2097152 | tf_op jit(solution)/shard_map/all_to_all | solution.py:182
  93.1 6.0 %copy-start.3 = (s32[256]{0:T(256)S(1)}, s32[256]{0:T(256)}, u32[]{:S(2)}) copy-start(s32[256]{0:T(256)} %slot_ref.1) | copy-start | bytes 3076
  93.1 6.0 %copy-start.4 = (s32[256]{0:T(256)S(1)}, s32[256]{0:T(256)}, u32[]{:S(2)}) copy-start(s32[256]{0:T(256)} %dst_ref.1) | copy-start | bytes 3076
  99.1 1.9 %copy-start.1 = (bf16[96,128,128]{2,1,0:T(8,128)(2,1)S(1)}, bf16[96,128,128]{2,1,0:T(8,128)(2,1)}, u32[]{:S(2)}) copy-start(bf16[96,128,128]{2,1,0:T(8,128)(2,1)} %all_to_all.15.recv) | copy-start | bytes 9437188
  101.0 3.4 %copy-start.2 = (bf16[256,128,128]{2,1,0:T(8,128)(2,1)S(1)}, bf16[256,128,128]{2,1,0:T(8,128)(2,1)}, u32[]{:S(2)}) copy-start(bf16[256,128,128]{2,1,0:T(8,128)(2,1)} %vals.1) | copy-start | bytes 25165828
  112.2 41.9 %copy-start.10 = (f32[1024]{0:T(1024)S(1)}, f32[1024]{0:T(1024)}, u32[]{:S(2)}) copy-start(f32[1024]{0:T(1024)} %param.20) | copy-start | bytes 12292
  122.2 31.9 %copy-start.5 = (bf16[1024,1024]{1,0:T(8,128)(2,1)S(1)}, bf16[1024,1024]{1,0:T(8,128)(2,1)}, u32[]{:S(2)}) copy-start(bf16[1024,1024]{1,0:T(8,128)(2,1)} %w2.1) | copy-start | bytes 6291460
  154.1 1.6 copy-start.6
  155.7 1.6 copy-start.7
  157.3 1.6 copy-start.11

commit v2 on v1

v2 whole, which is shorter than its diff:
```python
import jax
import jax.numpy as jnp
from jax import lax
from jax.experimental import pallas as pl
from jax.experimental.pallas import tpu as pltpu
from jax.sharding import PartitionSpec as P

CHUNK = 16
UNROLL = 16


def pack_tiles(feats, send_ids):
    row_tiles, side, cols = feats.shape
    slots = send_ids.shape[0]

    def body(ids, src, out, sem):
        def issue(i, _):
            pltpu.make_async_copy(src.at[ids[i]], out.at[i], sem).start()
            return 0

        lax.fori_loop(0, slots, issue, 0, unroll=8)
        pltpu.make_async_copy(out, out, sem).wait()

    return pl.pallas_call(
        body,
        grid_spec=pltpu.PrefetchScalarGridSpec(
            num_scalar_prefetch=1,
            grid=(1,),
            in_specs=[pl.BlockSpec((row_tiles, side, cols), lambda i, ids: (0, 0, 0))],
            out_specs=pl.BlockSpec(memory_space=pl.ANY),
            scratch_shapes=[pltpu.SemaphoreType.DMA],
        ),
        out_shape=jax.ShapeDtypeStruct((slots, side, cols), feats.dtype),
        compiler_params=pltpu.CompilerParams(vmem_limit_bytes=56 << 20),
        name="pack_tiles",
    )(send_ids, feats)


def own_pieces(feats, me, groups):
    row_tiles, side, cols = feats.shape
    per = row_tiles // groups
    half = groups // 2

    def body(me_ref, src, far, *near):
        for m in range(half):
            near[m][...] = src[pl.ds((me_ref[0] ^ (2 * m)) * per, per)]
            far[m] = src[pl.ds((me_ref[0] ^ (2 * m + 1)) * per, per)]

    piece = (per, side, cols)
    shapes = [(half,) + piece] + [piece] * half
    made = pl.pallas_call(
        body,
        grid_spec=pltpu.PrefetchScalarGridSpec(
            num_scalar_prefetch=1,
            grid=(1,),
            in_specs=[pl.BlockSpec((row_tiles, side, cols), lambda i, *_: (0, 0, 0))],
            out_specs=[pl.BlockSpec(n, lambda i, *_, z=len(n): (0,) * z) for n in shapes],
        ),
        out_shape=[jax.ShapeDtypeStruct(n, feats.dtype) for n in shapes],
        name="own_pieces",
    )(me, feats)
    return made[0], made[1:]


def aggregate(received, tile_vals, after, src_slot, dst_tile, tile_count, me, row_tiles, groups):
    slots, side, cols = received.shape
    entries = tile_vals.shape[0]
    levels = pl.cdiv(entries, slots)
    tail = entries - (levels - 1) * slots
    chunks = slots // CHUNK
    per = row_tiles // groups

    def copies(vals, store, sems, chunk):
        base = chunk * CHUNK
        out = []
        for level in range(levels):
            if level == levels - 1 and base >= tail:
                continue
            out.append(
                pltpu.make_async_copy(
                    vals.at[pl.ds(level * slots + base, CHUNK)],
                    store.at[pl.ds(base, CHUNK), level],
                    sems.at[chunk, level],
                )
            )
        return out

    def body(slot_ref, dst_ref, count_ref, me_ref, recv_hbm, vals, _, *rest):
        pieces, (recv, store, acc, sems, recv_sem) = rest[:groups], rest[groups:]
        arrive = pltpu.make_async_copy(recv_hbm, recv, recv_sem)
        arrive.start()
        for chunk in range(chunks):
            for copy in copies(vals, store, sems, chunk):
                copy.start()
        acc[...] = jnp.zeros_like(acc)
        count = count_ref[0]
        arrive.wait()
        for chunk in range(chunks):
            waits = copies(vals, store, sems, chunk)
            for copy in waits:
                copy.wait()
            live_levels = len(waits)

            def step(turn, _):
                for k in range(UNROLL):
                    j = chunk * CHUNK + turn * UNROLL + k
                    source = recv[slot_ref[j]]
                    left = store[j, :live_levels].reshape(live_levels * side, side)
                    product = jnp.dot(left, source, preferred_element_type=jnp.float32)
                    for level in range(live_levels):
                        i = j + level * slots
                        place = jnp.where(i < count, dst_ref[i], row_tiles)
                        acc[place] += product[level * side : (level + 1) * side]
                return 0

            lax.fori_loop(0, CHUNK // UNROLL, step, 0)
        for k in range(groups):
            there = (me_ref[0] ^ k) * per
            for tile in range(per):
                pieces[k][tile] = acc[there + tile].astype(pieces[k].dtype)

    return pl.pallas_call(
        body,
        grid_spec=pltpu.PrefetchScalarGridSpec(
            num_scalar_prefetch=4,
            grid=(1,),
            in_specs=[
                pl.BlockSpec(memory_space=pl.ANY),
                pl.BlockSpec(memory_space=pl.ANY),
                pl.BlockSpec(memory_space=pltpu.VMEM),
            ],
            out_specs=[pl.BlockSpec((per, side, cols), lambda i, *_: (0, 0, 0))] * groups,
            scratch_shapes=[
                pltpu.VMEM((slots, side, cols), received.dtype),
                pltpu.VMEM((slots, levels, side, side), tile_vals.dtype),
                pltpu.VMEM((row_tiles + 1, side, cols), jnp.float32),
                pltpu.SemaphoreType.DMA((chunks, levels)),
                pltpu.SemaphoreType.DMA,
            ],
        ),
        out_shape=[jax.ShapeDtypeStruct((per, side, cols), received.dtype)] * groups,
        compiler_params=pltpu.CompilerParams(vmem_limit_bytes=52 << 20),
        cost_estimate=pl.CostEstimate(
            flops=8 * entries * side * side * cols,
            bytes_accessed=entries * side * side * 2 + (slots + row_tiles) * side * cols * 2,
            transcendentals=0,
        ),
        name="aggregate",
    )(src_slot, dst_tile, tile_count, me, received, tile_vals, after)


def finish(agg, inputs, me, g_target, w_fwd, b_fwd, w_inv1, b_inv1, w_inv2, b_inv2):
    groups = len(agg)
    rows, cols = agg[0].shape
    width = groups * cols
    block = 256

    def body(me_ref, *refs):
        agg_refs, in_refs = refs[:groups], refs[groups : 2 * groups]
        gt_ref, wf, bf, w1, b1, w2, b2, hid_ref, out_ref, rows_agg, rows_in = refs[2 * groups :]
        for k in range(groups):
            where = pl.ds(pl.multiple_of((me_ref[0] ^ k) * cols, cols), cols)
            rows_agg[:, where] = agg_refs[k][...]
            rows_in[:, where] = in_refs[k][...]
        hidden = jnp.tanh(
            jnp.dot(rows_agg[...], wf[...], preferred_element_type=jnp.float32) + bf[...]
        )
        hidden = hidden.astype(hid_ref.dtype)
        hid_ref[...] = hidden
        inner = jnp.tanh(jnp.dot(hidden, w1[...], preferred_element_type=jnp.float32) + b1[...])
        inner = inner.astype(hid_ref.dtype)
        back = jnp.tanh(jnp.dot(inner, w2[...], preferred_element_type=jnp.float32) + b2[...])
        out_ref[...] = (rows_in[...].astype(jnp.float32) + gt_ref[...] - back).astype(out_ref.dtype)

    piece = pl.BlockSpec((block, cols), lambda i, *_: (i, 0))
    whole = pl.BlockSpec((block, width), lambda i, *_: (i, 0))
    weight = pl.BlockSpec((width, width), lambda i, *_: (0, 0))
    bias = pl.BlockSpec((1, width), lambda i, *_: (0, 0))
    return pl.pallas_call(
        body,
        grid_spec=pltpu.PrefetchScalarGridSpec(
            num_scalar_prefetch=1,
            grid=(rows // block,),
            in_specs=[piece] * (2 * groups) + [whole, weight, bias, weight, bias, weight, bias],
            out_specs=[whole, whole],
            scratch_shapes=[pltpu.VMEM((block, width), agg[0].dtype)] * 2,
        ),
        out_shape=[jax.ShapeDtypeStruct((rows, width), agg[0].dtype)] * 2,
        compiler_params=pltpu.CompilerParams(vmem_limit_bytes=40 << 20),
        cost_estimate=pl.CostEstimate(
            flops=6 * rows * width * width,
            bytes_accessed=6 * width * width + 12 * rows * width,
            transcendentals=3 * rows * width,
        ),
        name="finish",
    )(me, *agg, *inputs, g_target, w_fwd, b_fwd[None], w_inv1, b_inv1[None], w_inv2, b_inv2[None])


def exchange(pieces, groups):
    order = [k for k in range(groups) if k % 2] + [k for k in range(2, groups, 2)]
    back = [pieces[0]] + [None] * (groups - 1)
    for k in order:
        back[k] = lax.ppermute(pieces[k], "section", [(s, s ^ k) for s in range(groups)])
    return back


def swap(piece, k, groups):
    return lax.ppermute(piece, "section", [(s, s ^ k) for s in range(groups)])


def per_device(
    feats,
    tile_vals,
    src_slot,
    dst_tile,
    tile_count,
    send_tile,
    w_fwd,
    b_fwd,
    w_inv1,
    b_inv1,
    w_inv2,
    b_inv2,
    target,
):
    node_rows, feat_cols = feats.shape
    side = tile_vals.shape[1]
    row_tiles = node_rows // side
    rows = target.shape[0]
    groups = node_rows // rows
    me = lax.axis_index("section").astype(jnp.int32)[None]
    tiles = feats.reshape(row_tiles, side, feat_cols)
    outgoing = pack_tiles(tiles, send_tile[0])
    received = lax.all_to_all(outgoing, "dom", split_axis=0, concat_axis=0, tiled=True)
    inner = jnp.tanh(jnp.dot(target, w_inv1, preferred_element_type=jnp.float32) + b_inv1).astype(
        jnp.bfloat16
    )
    g_target = jnp.tanh(jnp.dot(inner, w_inv2, preferred_element_type=jnp.float32) + b_inv2)
    far, near = own_pieces(tiles, me, groups)
    near = [near[0]] + [swap(near[m], 2 * m, groups) for m in range(1, groups // 2)]
    far, after = lax.optimization_barrier((far, received[0, :8] + g_target[:8, :feat_cols]))
    far = swap(far, 1, groups)
    agg = aggregate(
        received, tile_vals, after, src_slot, dst_tile, tile_count, me, row_tiles, groups
    )
    input_rows = [near[0], far[0]]
    for m in range(1, groups // 2):
        input_rows += [near[m], swap(far[m], 2 * m, groups)]
    agg_rows = exchange(agg, groups)
    flat = lambda pieces: [p.reshape(rows, feat_cols) for p in pieces]
    hidden, shifted = finish(
        flat(agg_rows), flat(input_rows), me, g_target, w_fwd, b_fwd, w_inv1, b_inv1, w_inv2, b_inv2
    )
    return (hidden, shifted)


def solution(mesh):
    placed = (
        P("dom", "section"),
        P("dom", None, None),
        P("dom"),
        P("dom"),
        P("dom"),
        P("dom", None),
        P(),
        P(),
        P(),
        P(),
        P(),
        P(),
        P(("dom", "section"), None),
    )
    return jax.shard_map(
        per_device,
        mesh=mesh,
        in_specs=placed,
        out_specs=(P(("dom", "section"), None), P(("dom", "section"), None)),
        check_vma=False,
    )
```

time: 164 us -> 152 us (0.927)
  blocking collectives: 112 us -> 0 us
  waiting for transfers between devices: 10 us -> 79.9 us
  starting transfers between devices: 8.36 us -> 45.3 us
  local copies, waits for them, and re-layouts: 10.1 us -> 0.11 us
  Pallas kernels: 16.1 us -> 19.7 us
    all_to_all x2 -> x0, blocking collectives: 112 us -> none  [the longest x1 79.7 us: per_device(): lax.all_to_all(outgoing, 'dom', split_axis=0, concat_axis=0, tiled=True)]
    all_to_all x1, waiting for transfers between devices: 10 us -> 64 us  [per_device(): lax.all_to_all(outgoing, 'dom', split_axis=0, concat_axis=0, tiled=True)]
    ppermute x0 -> x14, starting transfers between devices: none -> 36.3 us  [the longest x7 22.3 us: exchange(): lax.ppermute(pieces[k], 'section', [(s, s ^ k) for s in range(groups)])]
    ppermute x0 -> x14, waiting for transfers between devices: none -> 15.9 us  [the longest x7 9.21 us: swap(): return lax.ppermute(piece, 'section', [(s, s ^ k) for s in range(groups)])]
    unnamed x24 -> x26, local copies, waits for them, and re-layouts: 10.1 us -> 0.08 us
    pallas_call x1 -> x2, Pallas kernels: 4.65 us -> 7.26 us  [the longest x1 5.02 us: finish(): pl.pallas_call(body, grid_spec=pltpu.PrefetchScalarGridSpec(num_scalar_pr...]
  transfers between devices with their start and end apart: 1 -> 15, of which waited for: 1 -> 9; matrix products, arithmetic and copies ran while one was open for 4% -> 3% of each run, Pallas kernels for 5% -> 7%
where the time goes in v2:
time: 152 us
  waiting for transfers between devices  79.9 us (53%)
  starting transfers between devices  45.3 us (30%)
  Pallas kernels  19.7 us (13%)
  matrix products  4.64 us (3%)
    all_to_all x1, waiting for transfers between devices, per_device(): lax.all_to_all(outgoing, 'dom', split_axis=0, concat_axis=0, tiled=True)  64 us
    ppermute x7, starting transfers between devices, exchange(): lax.ppermute(pieces[k], 'section', [(s, s ^ k) for s in range(groups)])  22.3 us
    ppermute x7, starting transfers between devices, swap(): return lax.ppermute(piece, 'section', [(s, s ^ k) for s in range(groups)])  14 us
    ppermute x7, waiting for transfers between devices, swap(): return lax.ppermute(piece, 'section', [(s, s ^ k) for s in range(groups)])  9.21 us
    all_to_all x1, starting transfers between devices, per_device(): lax.all_to_all(outgoing, 'dom', split_axis=0, concat_axis=0, tiled=True)  9.01 us
    pallas_call x1, Pallas kernels, aggregate(): pl.pallas_call(body, grid_spec=pltpu.PrefetchScalarGridSpec(num_scalar_pr...  8.7 us
    ppermute x7, waiting for transfers between devices, exchange(): lax.ppermute(pieces[k], 'section', [(s, s ^ k) for s in range(groups)])  6.73 us
    pallas_call x1, Pallas kernels, finish(): pl.pallas_call(body, grid_spec=pltpu.PrefetchScalarGridSpec(num_scalar_pr...  5.02 us
  transfers between devices with their start and end apart: 15, of which 9 were waited for; matrix products, arithmetic and copies ran while one was open for 3% of the time, Pallas kernels for 7%

profile of v2, /device:TPU:24, one launch (start us, length us, event | category | flops | bytes accessed | tf_op | source)
XLA Modules:
  0.0 151.8 jit_solution(7087186234647689246)
XLA Ops:
  0.6 3.7 %pack_tiles.1 = bf16[96,128,128]{2,1,0:T(8,128)(2,1)} custom-call(s32[96]{0:T(128)} %bitcast.57, bf16[32,128,128]{2,1,0:T(8,128)(2,1)} %bitcast.55), custom_call_target="tpu_custom_call" | custom-call | tf_op jit(solution)/shard_map/pack_tiles/pallas_call | solution.py:24
  4.4 9.0 %all-to-all-start = ((bf16[96,128,128]{2,1,0:T(8,128)(2,1)}), bf16[96,128,128]{2,1,0:T(8,128)(2,1)}, u32[]{:S(2)}, u32[]{:S(2)}) async-start(bf16[96,128,128]{2,1,0:T(8,128)(2,1)} %pack_tiles.1), calls=%async_computation | async-start | bytes 6291456 | tf_op jit(solution)/shard_map/all_to_all | solution.py:234
  13.4 2.2 %own_pieces.1 = (bf16[4,4,128,128]{3,2,1,0:T(8,128)(2,1)}, bf16[4,128,128]{2,1,0:T(8,128)(2,1)}, bf16[4,128,128]{2,1,0:T(8,128)(2,1)}, bf16[4,128,128]{2,1,0:T(8,128)(2,1)}, bf16[4,128,128]{2,1,0:T(8,128)(2,1)}) custom-call(s32[1]{0:T(128)} %bitcast.me_ref, bf16[32,128,128]{2,1,0:T(8,128)(2,1)} %bitcast.56), custom_call_target="tpu_custom_call" | custom-call | tf_op jit(solution)/shard_map/own_pieces/pallas_call | solution.py:51
  15.7 4.6 %add_tanh_fusion.refs_16_ = f32[512,1024]{1,0:T(8,128)S(1)} fusion(bf16[1024,1024]{1,0:T(8,128)(2,1)} %refs_21_.1, f32[1024]{0:T(1024)S(1)} %copy-done.5, bf16[512,1024]{1,0:T(8,128)(2,1)S(1)} %copy-done, bf16[1024,1024]{1,0:T(8,128)(2,1)} %refs_19_.1, f32[1024]{0:T(1024)S(1)} %copy-done.6), kind=kOutput, calls=%fused_computation | convolution fusion | flops 2149056512 | bytes 7348224 | tf_op jit(solution)/shard_map/dot_general | solution.py:238
  20.4 64.0 %all-to-all-done.recv_hbm = bf16[96,128,128]{2,1,0:T(8,128)(2,1)} async-done(((bf16[96,128,128]{2,1,0:T(8,128)(2,1)}), bf16[96,128,128]{2,1,0:T(8,128)(2,1)}, u32[]{:S(2)}, u32[]{:S(2)}) %all-to-all-start) | async-done | bytes 3145760 | tf_op jit(solution)/shard_map/all_to_all | solution.py:234
  84.4 0.7 slice_add_fusion._
  85.0 4.5 %collective-permute-start.7 = (bf16[4,4,128,128]{3,2,1,0:T(8,128)(2,1)}, bf16[4,4,128,128]{3,2,1,0:T(8,128)(2,1)S(1)}, u32[]{:S(2)}, u32[]{:S(2)}) collective-permute-start(bf16[4,4,128,128]{3,2,1,0:T(8,128)(2,1)} %get-tuple-element.28), channel_id=1, source_target_pairs={{0,1},{1,0},{2,3},{3,2},{4,5},{5,4},{6,7},{7,6},{8,9},{9,8},{10,11... | collective-permute-start | bytes 1572872 | tf_op jit(solution)/shard_map/ppermute | solution.py:208
  89.5 1.5 collective-permute-start.8
  91.0 2.7 %collective-permute-start.10 = (bf16[4,128,128]{2,1,0:T(8,128)(2,1)S(1)}, bf16[4,128,128]{2,1,0:T(8,128)(2,1)S(1)}, u32[]{:S(2)}, u32[]{:S(2)}) collective-permute-start(bf16[4,128,128]{2,1,0:T(8,128)(2,1)S(1)} %copy-done.11), channel_id=1, source_target_pairs={{0,4},{1,5},{2,6},{3,7},{4,0},{5,1},{6,2},{7,3},{8,12},{9,13},{10,... | collective-permute-start | bytes 393224 | tf_op jit(solution)/shard_map/ppermute | solution.py:208
  95.0 8.7 %aggregate.1 = (bf16[4,128,128]{2,1,0:T(8,128)(2,1)S(1)}, bf16[4,128,128]{2,1,0:T(8,128)(2,1)S(1)}, bf16[4,128,128]{2,1,0:T(8,128)(2,1)S(1)}, bf16[4,128,128]{2,...) custom-call(s32[256]{0:T(256)S(1)} %copy-done.8, ...), custom_call_target="tpu_custom_call" | custom-call | flops 4294967296 | bytes 12582912 | tf_op jit(solution)/shard_map/aggregate/pallas_call | solution.py:122
  103.7 1.5 %collective-permute-start = (bf16[4,128,128]{2,1,0:T(8,128)(2,1)S(1)}, bf16[4,128,128]{2,1,0:T(8,128)(2,1)S(1)}, u32[]{:S(2)}, u32[]{:S(2)}) collective-permute-start(bf16[4,128,128]{2,1,0:T(8,128)(2,1)S(1)} %get-tuple-element.20), channel_id=1, source_target_pairs={{0,1},{1,0},{2,3},{3,2},{4,5},{5,4},{6,7},{7,6},{8,9},{9,8},{10,11... | collective-permute-start | bytes 393224 | tf_op jit(solution)/shard_map/ppermute | solution.py:203
  105.5 5.7 %collective-permute-start.2 = (bf16[4,128,128]{2,1,0:T(8,128)(2,1)S(1)}, bf16[4,128,128]{2,1,0:T(8,128)(2,1)S(1)}, u32[]{:S(2)}, u32[]{:S(2)}) collective-permute-start(bf16[4,128,128]{2,1,0:T(8,128)(2,1)S(1)} %get-tuple-element.22), channel_id=1, source_target_pairs={{0,3},{1,2},{2,1},{3,0},{4,7},{5,6},{6,5},{7,4},{8,11},{9,10},{10,... | collective-permute-start | bytes 393224 | tf_op jit(solution)/shard_map/ppermute | solution.py:203
  111.2 2.3 %collective-permute-start.3 = (bf16[4,128,128]{2,1,0:T(8,128)(2,1)S(1)}, bf16[4,128,128]{2,1,0:T(8,128)(2,1)S(1)}, u32[]{:S(2)}, u32[]{:S(2)}) collective-permute-start(bf16[4,128,128]{2,1,0:T(8,128)(2,1)S(1)} %get-tuple-element.23), channel_id=1, source_target_pairs={{0,4},{1,5},{2,6},{3,7},{4,0},{5,1},{6,2},{7,3},{8,12},{9,13},{10,... | collective-permute-start | bytes 393224 | tf_op jit(solution)/shard_map/ppermute | solution.py:203
  113.5 6.7 %collective-permute-done.7 = bf16[4,4,128,128]{3,2,1,0:T(8,128)(2,1)S(1)} collective-permute-done((bf16[4,4,128,128]{3,2,1,0:T(8,128)(2,1)}, bf16[4,4,128,128]{3,2,1,0:T(8,128)(2,1)S(1)}, u32[]{:S(2)}, u32[]{:S(2)}) %collective-permute-start.7) | collective-permute-done | bytes 524320 | tf_op jit(solution)/shard_map/ppermute | solution.py:208
  120.2 7.2 %collective-permute-start.4 = (bf16[4,128,128]{2,1,0:T(8,128)(2,1)S(1)}, bf16[4,128,128]{2,1,0:T(8,128)(2,1)S(1)}, u32[]{:S(2)}, u32[]{:S(2)}) collective-permute-start(bf16[4,128,128]{2,1,0:T(8,128)(2,1)S(1)} %get-tuple-element.24), channel_id=1, source_target_pairs={{0,5},{1,4},{2,7},{3,6},{4,1},{5,0},{6,3},{7,2},{8,13},{9,12},{10,... | collective-permute-start | bytes 393224 | tf_op jit(solution)/shard_map/ppermute | solution.py:203
  127.5 0.6 collective-permute-done
  128.0 4.2 %collective-permute-start.5 = (bf16[4,128,128]{2,1,0:T(8,128)(2,1)S(1)}, bf16[4,128,128]{2,1,0:T(8,128)(2,1)S(1)}, u32[]{:S(2)}, u32[]{:S(2)}) collective-permute-start(bf16[4,128,128]{2,1,0:T(8,128)(2,1)S(1)} %get-tuple-element.25), channel_id=1, source_target_pairs={{0,6},{1,7},{2,4},{3,5},{4,2},{5,3},{6,0},{7,1},{8,14},{9,15},{10,... | collective-permute-start | bytes 393224 | tf_op jit(solution)/shard_map/ppermute | solution.py:203
  132.3 1.1 collective-permute-start.6
  134.1 4.0 %collective-permute-start.11 = (bf16[4,128,128]{2,1,0:T(8,128)(2,1)S(1)}, bf16[4,128,128]{2,1,0:T(8,128)(2,1)S(1)}, u32[]{:S(2)}, u32[]{:S(2)}) collective-permute-start(bf16[4,128,128]{2,1,0:T(8,128)(2,1)S(1)} %get-tuple-element.33), channel_id=1, source_target_pairs={{0,4},{1,5},{2,6},{3,7},{4,0},{5,1},{6,2},{7,3},{8,12},{9,13},{10,... | collective-permute-start | bytes 393224 | tf_op jit(solution)/shard_map/ppermute | solution.py:208
  138.1 0.5 collective-permute-done.4
  138.9 2.8 %collective-permute-done.5 = bf16[4,128,128]{2,1,0:T(8,128)(2,1)S(1)} collective-permute-done((bf16[4,128,128]{2,1,0:T(8,128)(2,1)S(1)}, bf16[4,128,128]{2,1,0:T(8,128)(2,1)S(1)}, u32[]{:S(2)}, u32[]{:S(2)}) %collective-permute-start.5) | collective-permute-done | bytes 131104 | tf_op jit(solution)/shard_map/ppermute | solution.py:203
  141.7 2.6 %collective-permute-done.6 = bf16[4,128,128]{2,1,0:T(8,128)(2,1)S(1)} collective-permute-done((bf16[4,128,128]{2,1,0:T(8,128)(2,1)S(1)}, bf16[4,128,128]{2,1,0:T(8,128)(2,1)S(1)}, u32[]{:S(2)}, u32[]{:S(2)}) %collective-permute-start.6) | collective-permute-done | bytes 131104 | tf_op jit(solution)/shard_map/ppermute | solution.py:203
  144.7 2.1 %collective-permute-done.13 = bf16[4,128,128]{2,1,0:T(8,128)(2,1)S(1)} collective-permute-done((bf16[4,128,128]{2,1,0:T(8,128)(2,1)S(1)}, bf16[4,128,128]{2,1,0:T(8,128)(2,1)S(1)}, u32[]{:S(2)}, u32[]{:S(2)}) %collective-permute-start.13) | collective-permute-done | bytes 131104 | tf_op jit(solution)/shard_map/ppermute | solution.py:208
  146.8 5.0 %finish.1 = (bf16[512,1024]{1,0:T(8,128)(2,1)}, bf16[512,1024]{1,0:T(8,128)(2,1)}) custom-call(s32[1]{0:T(128)} %bitcast.me_ref, bf16[512,128]{1,0:T(8,128)(2,1)S(1)} %bitcast.54, bf16[512,128]{1,0:T(8,128)(2,1)S(1)} %bitcast.41, bf16[512,128]{1,0:T(8,128)(2,1)S(1)} %bitcast.42, bf16[512,128]{1,0:T(8,128)(2,1)S(1)} %bitcast.43, ...), custom_call_target="tpu_custom_call" | custom-call | flops 3221225472 | bytes 12582912 | tf_op jit(solution)/shard_map/finish/pallas_call | solution.py:179
  (39 shorter events, 2.3 us)
Async XLA Ops:
  4.4 80.0 %all-to-all-start = ((bf16[96,128,128]{2,1,0:T(8,128)(2,1)}), bf16[96,128,128]{2,1,0:T(8,128)(2,1)}, u32[]{:S(2)}, u32[]{:S(2)}) async-start(bf16[96,128,128]{2,1,0:T(8,128)(2,1)} %pack_tiles.1), calls=%async_computation | async-start | bytes 6291456 | tf_op jit(solution)/shard_map/all_to_all | solution.py:234
  15.7 73.9 %copy-start.12 = (bf16[4,128,128]{2,1,0:T(8,128)(2,1)S(1)}, bf16[4,128,128]{2,1,0:T(8,128)(2,1)}, u32[]{:S(2)}) copy-start(bf16[4,128,128]{2,1,0:T(8,128)(2,1)} %get-tuple-element.29) | copy-start | bytes 393220
  15.7 75.4 %copy-start.11 = (bf16[4,128,128]{2,1,0:T(8,128)(2,1)S(1)}, bf16[4,128,128]{2,1,0:T(8,128)(2,1)}, u32[]{:S(2)}) copy-start(bf16[4,128,128]{2,1,0:T(8,128)(2,1)} %get-tuple-element.30) | copy-start | bytes 393220
  15.7 78.1 %copy-start.10 = (bf16[4,128,128]{2,1,0:T(8,128)(2,1)S(1)}, bf16[4,128,128]{2,1,0:T(8,128)(2,1)}, u32[]{:S(2)}) copy-start(bf16[4,128,128]{2,1,0:T(8,128)(2,1)} %get-tuple-element.31) | copy-start | bytes 393220
  15.7 79.2 %copy-start.8 = (s32[256]{0:T(256)S(1)}, s32[256]{0:T(256)}, u32[]{:S(2)}) copy-start(s32[256]{0:T(256)} %slot_ref.1) | copy-start | bytes 3076
  15.7 79.2 %copy-start.9 = (s32[256]{0:T(256)S(1)}, s32[256]{0:T(256)}, u32[]{:S(2)}) copy-start(s32[256]{0:T(256)} %dst_ref.1) | copy-start | bytes 3076
  85.0 35.2 %collective-permute-start.7 = (bf16[4,4,128,128]{3,2,1,0:T(8,128)(2,1)}, bf16[4,4,128,128]{3,2,1,0:T(8,128)(2,1)S(1)}, u32[]{:S(2)}, u32[]{:S(2)}) collective-permute-start(bf16[4,4,128,128]{3,2,1,0:T(8,128)(2,1)} %get-tuple-element.28), channel_id=1, source_target_pairs={{0,1},{1,0},{2,3},{3,2},{4,5},{5,4},{6,7},{7,6},{8,9},{9,8},{10,11... | collective-permute-start | bytes 1572872 | tf_op jit(solution)/shard_map/ppermute | solution.py:208
  89.5 15.7 %collective-permute-start.8 = (bf16[4,128,128]{2,1,0:T(8,128)(2,1)S(1)}, bf16[4,128,128]{2,1,0:T(8,128)(2,1)S(1)}, u32[]{:S(2)}, u32[]{:S(2)}) collective-permute-start(bf16[4,128,128]{2,1,0:T(8,128)(2,1)S(1)} %copy-done.12), channel_id=1, source_target_pairs={{0,2},{1,3},{2,0},{3,1},{4,6},{5,7},{6,4},{7,5},{8,10},{9,11},{10,... | collective-permute-start | bytes 393224 | tf_op jit(solution)/shard_map/ppermute | solution.py:208
  91.0 14.5 %collective-permute-start.10 = (bf16[4,128,128]{2,1,0:T(8,128)(2,1)S(1)}, bf16[4,128,128]{2,1,0:T(8,128)(2,1)S(1)}, u32[]{:S(2)}, u32[]{:S(2)}) collective-permute-start(bf16[4,128,128]{2,1,0:T(8,128)(2,1)S(1)} %copy-done.11), channel_id=1, source_target_pairs={{0,4},{1,5},{2,6},{3,7},{4,0},{5,1},{6,2},{7,3},{8,12},{9,13},{10,... | collective-permute-start | bytes 393224 | tf_op jit(solution)/shard_map/ppermute | solution.py:208
  93.8 17.4 %collective-permute-start.12 = (bf16[4,128,128]{2,1,0:T(8,128)(2,1)S(1)}, bf16[4,128,128]{2,1,0:T(8,128)(2,1)S(1)}, u32[]{:S(2)}, u32[]{:S(2)}) collective-permute-start(bf16[4,128,128]{2,1,0:T(8,128)(2,1)S(1)} %copy-done.10), channel_id=1, source_target_pairs={{0,6},{1,7},{2,4},{3,5},{4,2},{5,3},{6,0},{7,1},{8,14},{9,15},{10,... | collective-permute-start | bytes 393224 | tf_op jit(solution)/shard_map/ppermute | solution.py:208
  94.9 51.9 %copy-start.1 = (bf16[1024,1024]{1,0:T(8,128)(2,1)S(1)}, bf16[1024,1024]{1,0:T(8,128)(2,1)}, u32[]{:S(2)}) copy-start(bf16[1024,1024]{1,0:T(8,128)(2,1)} %refs_21_.1) | copy-start | bytes 6291460
  94.9 51.9 %copy-start.2 = (bf16[1024,1024]{1,0:T(8,128)(2,1)S(1)}, bf16[1024,1024]{1,0:T(8,128)(2,1)}, u32[]{:S(2)}) copy-start(bf16[1024,1024]{1,0:T(8,128)(2,1)} %refs_19_.1) | copy-start | bytes 6291460
  94.9 51.9 %copy-start.3 = (bf16[1024,1024]{1,0:T(8,128)(2,1)S(1)}, bf16[1024,1024]{1,0:T(8,128)(2,1)}, u32[]{:S(2)}) copy-start(bf16[1024,1024]{1,0:T(8,128)(2,1)} %refs_17_.1) | copy-start | bytes 6291460
  95.0 51.8 %copy-start.4 = (bf16[4,128,128]{2,1,0:T(8,128)(2,1)S(1)}, bf16[4,128,128]{2,1,0:T(8,128)(2,1)}, u32[]{:S(2)}) copy-start(bf16[4,128,128]{2,1,0:T(8,128)(2,1)} %get-tuple-element.27) | copy-start | bytes 393220
  103.7 24.4 %collective-permute-start = (bf16[4,128,128]{2,1,0:T(8,128)(2,1)S(1)}, bf16[4,128,128]{2,1,0:T(8,128)(2,1)S(1)}, u32[]{:S(2)}, u32[]{:S(2)}) collective-permute-start(bf16[4,128,128]{2,1,0:T(8,128)(2,1)S(1)} %get-tuple-element.20), channel_id=1, source_target_pairs={{0,1},{1,0},{2,3},{3,2},{4,5},{5,4},{6,7},{7,6},{8,9},{9,8},{10,11... | collective-permute-start | bytes 393224 | tf_op jit(solution)/shard_map/ppermute | solution.py:203
  105.2 27.0 %collective-permute-start.1 = (bf16[4,128,128]{2,1,0:T(8,128)(2,1)S(1)}, bf16[4,128,128]{2,1,0:T(8,128)(2,1)S(1)}, u32[]{:S(2)}, u32[]{:S(2)}) collective-permute-start(bf16[4,128,128]{2,1,0:T(8,128)(2,1)S(1)} %get-tuple-element.21), channel_id=1, source_target_pairs={{0,2},{1,3},{2,0},{3,1},{4,6},{5,7},{6,4},{7,5},{8,10},{9,11},{10,... | collective-permute-start | bytes 393224 | tf_op jit(solution)/shard_map/ppermute | solution.py:203
  105.5 28.1 %collective-permute-start.2 = (bf16[4,128,128]{2,1,0:T(8,128)(2,1)S(1)}, bf16[4,128,128]{2,1,0:T(8,128)(2,1)S(1)}, u32[]{:S(2)}, u32[]{:S(2)}) collective-permute-start(bf16[4,128,128]{2,1,0:T(8,128)(2,1)S(1)} %get-tuple-element.22), channel_id=1, source_target_pairs={{0,3},{1,2},{2,1},{3,0},{4,7},{5,6},{6,5},{7,4},{8,11},{9,10},{10,... | collective-permute-start | bytes 393224 | tf_op jit(solution)/shard_map/ppermute | solution.py:203
  111.2 23.0 %collective-permute-start.3 = (bf16[4,128,128]{2,1,0:T(8,128)(2,1)S(1)}, bf16[4,128,128]{2,1,0:T(8,128)(2,1)S(1)}, u32[]{:S(2)}, u32[]{:S(2)}) collective-permute-start(bf16[4,128,128]{2,1,0:T(8,128)(2,1)S(1)} %get-tuple-element.23), channel_id=1, source_target_pairs={{0,4},{1,5},{2,6},{3,7},{4,0},{5,1},{6,2},{7,3},{8,12},{9,13},{10,... | collective-permute-start | bytes 393224 | tf_op jit(solution)/shard_map/ppermute | solution.py:203
  120.2 18.4 %collective-permute-start.4 = (bf16[4,128,128]{2,1,0:T(8,128)(2,1)S(1)}, bf16[4,128,128]{2,1,0:T(8,128)(2,1)S(1)}, u32[]{:S(2)}, u32[]{:S(2)}) collective-permute-start(bf16[4,128,128]{2,1,0:T(8,128)(2,1)S(1)} %get-tuple-element.24), channel_id=1, source_target_pairs={{0,5},{1,4},{2,7},{3,6},{4,1},{5,0},{6,3},{7,2},{8,13},{9,12},{10,... | collective-permute-start | bytes 393224 | tf_op jit(solution)/shard_map/ppermute | solution.py:203
  128.0 13.7 %collective-permute-start.5 = (bf16[4,128,128]{2,1,0:T(8,128)(2,1)S(1)}, bf16[4,128,128]{2,1,0:T(8,128)(2,1)S(1)}, u32[]{:S(2)}, u32[]{:S(2)}) collective-permute-start(bf16[4,128,128]{2,1,0:T(8,128)(2,1)S(1)} %get-tuple-element.25), channel_id=1, source_target_pairs={{0,6},{1,7},{2,4},{3,5},{4,2},{5,3},{6,0},{7,1},{8,14},{9,15},{10,... | collective-permute-start | bytes 393224 | tf_op jit(solution)/shard_map/ppermute | solution.py:203
  132.3 12.1 %collective-permute-start.6 = (bf16[4,128,128]{2,1,0:T(8,128)(2,1)S(1)}, bf16[4,128,128]{2,1,0:T(8,128)(2,1)S(1)}, u32[]{:S(2)}, u32[]{:S(2)}) collective-permute-start(bf16[4,128,128]{2,1,0:T(8,128)(2,1)S(1)} %get-tuple-element.26), channel_id=1, source_target_pairs={{0,7},{1,6},{2,5},{3,4},{4,3},{5,2},{6,1},{7,0},{8,15},{9,14},{10,... | collective-permute-start | bytes 393224 | tf_op jit(solution)/shard_map/ppermute | solution.py:203
  133.6 10.7 %collective-permute-start.9 = (bf16[4,128,128]{2,1,0:T(8,128)(2,1)S(1)}, bf16[4,128,128]{2,1,0:T(8,128)(2,1)S(1)}, u32[]{:S(2)}, u32[]{:S(2)}) collective-permute-start(bf16[4,128,128]{2,1,0:T(8,128)(2,1)S(1)} %get-tuple-element.34), channel_id=1, source_target_pairs={{0,2},{1,3},{2,0},{3,1},{4,6},{5,7},{6,4},{7,5},{8,10},{9,11},{10,... | collective-permute-start | bytes 393224 | tf_op jit(solution)/shard_map/ppermute | solution.py:208
  134.1 10.5 %collective-permute-start.11 = (bf16[4,128,128]{2,1,0:T(8,128)(2,1)S(1)}, bf16[4,128,128]{2,1,0:T(8,128)(2,1)S(1)}, u32[]{:S(2)}, u32[]{:S(2)}) collective-permute-start(bf16[4,128,128]{2,1,0:T(8,128)(2,1)S(1)} %get-tuple-element.33), channel_id=1, source_target_pairs={{0,4},{1,5},{2,6},{3,7},{4,0},{5,1},{6,2},{7,3},{8,12},{9,13},{10,... | collective-permute-start | bytes 393224 | tf_op jit(solution)/shard_map/ppermute | solution.py:208
  138.6 8.2 %collective-permute-start.13 = (bf16[4,128,128]{2,1,0:T(8,128)(2,1)S(1)}, bf16[4,128,128]{2,1,0:T(8,128)(2,1)S(1)}, u32[]{:S(2)}, u32[]{:S(2)}) collective-permute-start(bf16[4,128,128]{2,1,0:T(8,128)(2,1)S(1)} %get-tuple-element.32), channel_id=1, source_target_pairs={{0,6},{1,7},{2,4},{3,5},{4,2},{5,3},{6,0},{7,1},{8,14},{9,15},{10,... | collective-permute-start | bytes 393224 | tf_op jit(solution)/shard_map/ppermute | solution.py:208
  (4 other events, 89.4 us)

commit v3 on v2

--- a/solution.py
+++ b/solution.py
@@ -26,7 +26,7 @@
         grid_spec=pltpu.PrefetchScalarGridSpec(
             num_scalar_prefetch=1,
             grid=(1,),
-            in_specs=[pl.BlockSpec((row_tiles, side, cols), lambda i, ids: (0, 0, 0))],
+            in_specs=[pl.BlockSpec(memory_space=pl.ANY)],
             out_specs=pl.BlockSpec(memory_space=pl.ANY),
             scratch_shapes=[pltpu.SemaphoreType.DMA],
         ),

time: 152 us -> 246 us (1.62)
  Pallas kernels: 19.7 us -> 113 us
    pallas_call x1, Pallas kernels: 3.71 us -> 97.2 us  [pack_tiles(): pl.pallas_call(body, grid_spec=pltpu.PrefetchScalarGridSpec(num_scalar_pr...]
  transfers between devices with their start and end apart: 15 -> 15, of which waited for: 9 -> 9; matrix products, arithmetic and copies ran while one was open for 3% -> 2% of each run, Pallas kernels for 7% -> 4%
where the time goes in v3:
time: 246 us; the launch traced here: 245 us
  Pallas kernels  113 us (46%)
  waiting for transfers between devices  79.9 us (32%)
  starting transfers between devices  45.3 us (18%)
  matrix products  4.64 us (2%)
    pallas_call x1, Pallas kernels, pack_tiles(): pl.pallas_call(body, grid_spec=pltpu.PrefetchScalarGridSpec(num_scalar_pr...  97.2 us
    all_to_all x1, waiting for transfers between devices, per_device(): lax.all_to_all(outgoing, 'dom', split_axis=0, concat_axis=0, tiled=True)  64 us
    ppermute x7, starting transfers between devices, exchange(): lax.ppermute(pieces[k], 'section', [(s, s ^ k) for s in range(groups)])  22.3 us
    ppermute x7, starting transfers between devices, swap(): return lax.ppermute(piece, 'section', [(s, s ^ k) for s in range(groups)])  14 us
    ppermute x7, waiting for transfers between devices, swap(): return lax.ppermute(piece, 'section', [(s, s ^ k) for s in range(groups)])  9.22 us
    all_to_all x1, starting transfers between devices, per_device(): lax.all_to_all(outgoing, 'dom', split_axis=0, concat_axis=0, tiled=True)  9.01 us
    pallas_call x1, Pallas kernels, aggregate(): pl.pallas_call(body, grid_spec=pltpu.PrefetchScalarGridSpec(num_scalar_pr...  8.71 us
    ppermute x7, waiting for transfers between devices, exchange(): lax.ppermute(pieces[k], 'section', [(s, s ^ k) for s in range(groups)])  6.73 us
  transfers between devices with their start and end apart: 15, of which 9 were waited for; matrix products, arithmetic and copies ran while one was open for 2% of the time, Pallas kernels for 4%

profile of v3, /device:TPU:24, one launch (start us, length us, event | category | flops | bytes accessed | tf_op | source)
XLA Modules:
  0.0 245.3 jit_solution(18355378658873530306)
XLA Ops:
  0.6 97.2 %pack_tiles.1 = bf16[96,128,128]{2,1,0:T(8,128)(2,1)} custom-call(s32[96]{0:T(128)} %bitcast.57, bf16[32,128,128]{2,1,0:T(8,128)(2,1)} %bitcast.55), custom_call_target="tpu_custom_call" | custom-call | tf_op jit(solution)/shard_map/pack_tiles/pallas_call | solution.py:24
  97.9 9.0 %all-to-all-start = ((bf16[96,128,128]{2,1,0:T(8,128)(2,1)}), bf16[96,128,128]{2,1,0:T(8,128)(2,1)}, u32[]{:S(2)}, u32[]{:S(2)}) async-start(bf16[96,128,128]{2,1,0:T(8,128)(2,1)} %pack_tiles.1), calls=%async_computation | async-start | bytes 6291456 | tf_op jit(solution)/shard_map/all_to_all | solution.py:234
  106.9 2.2 own_pieces.1
  109.2 4.6 %add_tanh_fusion.refs_16_ = f32[512,1024]{1,0:T(8,128)S(1)} fusion(bf16[1024,1024]{1,0:T(8,128)(2,1)} %refs_21_.1, f32[1024]{0:T(1024)S(1)} %copy-done.5, bf16[512,1024]{1,0:T(8,128)(2,1)S(1)} %copy-done, bf16[1024,1024]{1,0:T(8,128)(2,1)} %refs_19_.1, f32[1024]{0:T(1024)S(1)} %copy-done.6), kind=kOutput, calls=%fused_computation | convolution fusion | flops 2149056512 | bytes 7348224 | tf_op jit(solution)/shard_map/dot_general | solution.py:238
  113.9 64.0 %all-to-all-done.recv_hbm = bf16[96,128,128]{2,1,0:T(8,128)(2,1)} async-done(((bf16[96,128,128]{2,1,0:T(8,128)(2,1)}), bf16[96,128,128]{2,1,0:T(8,128)(2,1)}, u32[]{:S(2)}, u32[]{:S(2)}) %all-to-all-start) | async-done | bytes 3145760 | tf_op jit(solution)/shard_map/all_to_all | solution.py:234
  177.8 0.7 slice_add_fusion._
  178.5 4.5 %collective-permute-start.7 = (bf16[4,4,128,128]{3,2,1,0:T(8,128)(2,1)}, bf16[4,4,128,128]{3,2,1,0:T(8,128)(2,1)S(1)}, u32[]{:S(2)}, u32[]{:S(2)}) collective-permute-start(bf16[4,4,128,128]{3,2,1,0:T(8,128)(2,1)} %get-tuple-element.28), channel_id=1, source_target_pairs={{0,1},{1,0},{2,3},{3,2},{4,5},{5,4},{6,7},{7,6},{8,9},{9,8},{10,11... | collective-permute-start | bytes 1572872 | tf_op jit(solution)/shard_map/ppermute | solution.py:208
  183.0 1.5 collective-permute-start.8
  184.5 2.7 %collective-permute-start.10 = (bf16[4,128,128]{2,1,0:T(8,128)(2,1)S(1)}, bf16[4,128,128]{2,1,0:T(8,128)(2,1)S(1)}, u32[]{:S(2)}, u32[]{:S(2)}) collective-permute-start(bf16[4,128,128]{2,1,0:T(8,128)(2,1)S(1)} %copy-done.11), channel_id=1, source_target_pairs={{0,4},{1,5},{2,6},{3,7},{4,0},{5,1},{6,2},{7,3},{8,12},{9,13},{10,... | collective-permute-start | bytes 393224 | tf_op jit(solution)/shard_map/ppermute | solution.py:208
  188.5 8.7 %aggregate.1 = (bf16[4,128,128]{2,1,0:T(8,128)(2,1)S(1)}, bf16[4,128,128]{2,1,0:T(8,128)(2,1)S(1)}, bf16[4,128,128]{2,1,0:T(8,128)(2,1)S(1)}, bf16[4,128,128]{2,...) custom-call(s32[256]{0:T(256)S(1)} %copy-done.8, ...), custom_call_target="tpu_custom_call" | custom-call | flops 4294967296 | bytes 12582912 | tf_op jit(solution)/shard_map/aggregate/pallas_call | solution.py:122
  197.2 1.5 collective-permute-start
  199.0 5.7 %collective-permute-start.2 = (bf16[4,128,128]{2,1,0:T(8,128)(2,1)S(1)}, bf16[4,128,128]{2,1,0:T(8,128)(2,1)S(1)}, u32[]{:S(2)}, u32[]{:S(2)}) collective-permute-start(bf16[4,128,128]{2,1,0:T(8,128)(2,1)S(1)} %get-tuple-element.22), channel_id=1, source_target_pairs={{0,3},{1,2},{2,1},{3,0},{4,7},{5,6},{6,5},{7,4},{8,11},{9,10},{10,... | collective-permute-start | bytes 393224 | tf_op jit(solution)/shard_map/ppermute | solution.py:203
  204.7 2.3 collective-permute-start.3
  207.0 6.7 %collective-permute-done.7 = bf16[4,4,128,128]{3,2,1,0:T(8,128)(2,1)S(1)} collective-permute-done((bf16[4,4,128,128]{3,2,1,0:T(8,128)(2,1)}, bf16[4,4,128,128]{3,2,1,0:T(8,128)(2,1)S(1)}, u32[]{:S(2)}, u32[]{:S(2)}) %collective-permute-start.7) | collective-permute-done | bytes 524320 | tf_op jit(solution)/shard_map/ppermute | solution.py:208
  213.7 7.2 %collective-permute-start.4 = (bf16[4,128,128]{2,1,0:T(8,128)(2,1)S(1)}, bf16[4,128,128]{2,1,0:T(8,128)(2,1)S(1)}, u32[]{:S(2)}, u32[]{:S(2)}) collective-permute-start(bf16[4,128,128]{2,1,0:T(8,128)(2,1)S(1)} %get-tuple-element.24), channel_id=1, source_target_pairs={{0,5},{1,4},{2,7},{3,6},{4,1},{5,0},{6,3},{7,2},{8,13},{9,12},{10,... | collective-permute-start | bytes 393224 | tf_op jit(solution)/shard_map/ppermute | solution.py:203
  221.0 0.6 collective-permute-done
  221.5 4.2 %collective-permute-start.5 = (bf16[4,128,128]{2,1,0:T(8,128)(2,1)S(1)}, bf16[4,128,128]{2,1,0:T(8,128)(2,1)S(1)}, u32[]{:S(2)}, u32[]{:S(2)}) collective-permute-start(bf16[4,128,128]{2,1,0:T(8,128)(2,1)S(1)} %get-tuple-element.25), channel_id=1, source_target_pairs={{0,6},{1,7},{2,4},{3,5},{4,2},{5,3},{6,0},{7,1},{8,14},{9,15},{10,... | collective-permute-start | bytes 393224 | tf_op jit(solution)/shard_map/ppermute | solution.py:203
  225.7 1.1 collective-permute-start.6
  227.6 4.0 %collective-permute-start.11 = (bf16[4,128,128]{2,1,0:T(8,128)(2,1)S(1)}, bf16[4,128,128]{2,1,0:T(8,128)(2,1)S(1)}, u32[]{:S(2)}, u32[]{:S(2)}) collective-permute-start(bf16[4,128,128]{2,1,0:T(8,128)(2,1)S(1)} %get-tuple-element.33), channel_id=1, source_target_pairs={{0,4},{1,5},{2,6},{3,7},{4,0},{5,1},{6,2},{7,3},{8,12},{9,13},{10,... | collective-permute-start | bytes 393224 | tf_op jit(solution)/shard_map/ppermute | solution.py:208
  231.6 0.5 collective-permute-done.4
  232.4 2.8 %collective-permute-done.5 = bf16[4,128,128]{2,1,0:T(8,128)(2,1)S(1)} collective-permute-done((bf16[4,128,128]{2,1,0:T(8,128)(2,1)S(1)}, bf16[4,128,128]{2,1,0:T(8,128)(2,1)S(1)}, u32[]{:S(2)}, u32[]{:S(2)}) %collective-permute-start.5) | collective-permute-done | bytes 131104 | tf_op jit(solution)/shard_map/ppermute | solution.py:203
  235.2 2.6 %collective-permute-done.6 = bf16[4,128,128]{2,1,0:T(8,128)(2,1)S(1)} collective-permute-done((bf16[4,128,128]{2,1,0:T(8,128)(2,1)S(1)}, bf16[4,128,128]{2,1,0:T(8,128)(2,1)S(1)}, u32[]{:S(2)}, u32[]{:S(2)}) %collective-permute-start.6) | collective-permute-done | bytes 131104 | tf_op jit(solution)/shard_map/ppermute | solution.py:203
  238.2 2.1 collective-permute-done.13
  240.3 5.0 %finish.1 = (bf16[512,1024]{1,0:T(8,128)(2,1)}, bf16[512,1024]{1,0:T(8,128)(2,1)}) custom-call(s32[1]{0:T(128)} %bitcast.me_ref, bf16[512,128]{1,0:T(8,128)(2,1)S(1)} %bitcast.54, bf16[512,128]{1,0:T(8,128)(2,1)S(1)} %bitcast.41, bf16[512,128]{1,0:T(8,128)(2,1)S(1)} %bitcast.42, bf16[512,128]{1,0:T(8,128)(2,1)S(1)} %bitcast.43, ...), custom_call_target="tpu_custom_call" | custom-call | flops 3221225472 | bytes 12582912 | tf_op jit(solution)/shard_map/finish/pallas_call | solution.py:179
  (39 shorter events, 2.3 us)
Async XLA Ops:
  0.6 108.5 %copy-start = (bf16[512,1024]{1,0:T(8,128)(2,1)S(1)}, bf16[512,1024]{1,0:T(8,128)(2,1)}, u32[]{:S(2)}) copy-start(bf16[512,1024]{1,0:T(8,128)(2,1)} %param.25) | copy-start | bytes 3145732
  97.9 80.0 %all-to-all-start = ((bf16[96,128,128]{2,1,0:T(8,128)(2,1)}), bf16[96,128,128]{2,1,0:T(8,128)(2,1)}, u32[]{:S(2)}, u32[]{:S(2)}) async-start(bf16[96,128,128]{2,1,0:T(8,128)(2,1)} %pack_tiles.1), calls=%async_computation | async-start | bytes 6291456 | tf_op jit(solution)/shard_map/all_to_all | solution.py:234
  109.1 73.9 %copy-start.12 = (bf16[4,128,128]{2,1,0:T(8,128)(2,1)S(1)}, bf16[4,128,128]{2,1,0:T(8,128)(2,1)}, u32[]{:S(2)}) copy-start(bf16[4,128,128]{2,1,0:T(8,128)(2,1)} %get-tuple-element.29) | copy-start | bytes 393220
  109.2 75.4 %copy-start.11 = (bf16[4,128,128]{2,1,0:T(8,128)(2,1)S(1)}, bf16[4,128,128]{2,1,0:T(8,128)(2,1)}, u32[]{:S(2)}) copy-start(bf16[4,128,128]{2,1,0:T(8,128)(2,1)} %get-tuple-element.30) | copy-start | bytes 393220
  109.2 78.1 %copy-start.10 = (bf16[4,128,128]{2,1,0:T(8,128)(2,1)S(1)}, bf16[4,128,128]{2,1,0:T(8,128)(2,1)}, u32[]{:S(2)}) copy-start(bf16[4,128,128]{2,1,0:T(8,128)(2,1)} %get-tuple-element.31) | copy-start | bytes 393220
  109.2 79.2 %copy-start.8 = (s32[256]{0:T(256)S(1)}, s32[256]{0:T(256)}, u32[]{:S(2)}) copy-start(s32[256]{0:T(256)} %slot_ref.1) | copy-start | bytes 3076
  109.2 79.2 %copy-start.9 = (s32[256]{0:T(256)S(1)}, s32[256]{0:T(256)}, u32[]{:S(2)}) copy-start(s32[256]{0:T(256)} %dst_ref.1) | copy-start | bytes 3076
  178.5 35.2 %collective-permute-start.7 = (bf16[4,4,128,128]{3,2,1,0:T(8,128)(2,1)}, bf16[4,4,128,128]{3,2,1,0:T(8,128)(2,1)S(1)}, u32[]{:S(2)}, u32[]{:S(2)}) collective-permute-start(bf16[4,4,128,128]{3,2,1,0:T(8,128)(2,1)} %get-tuple-element.28), channel_id=1, source_target_pairs={{0,1},{1,0},{2,3},{3,2},{4,5},{5,4},{6,7},{7,6},{8,9},{9,8},{10,11... | collective-permute-start | bytes 1572872 | tf_op jit(solution)/shard_map/ppermute | solution.py:208
  183.0 15.7 %collective-permute-start.8 = (bf16[4,128,128]{2,1,0:T(8,128)(2,1)S(1)}, bf16[4,128,128]{2,1,0:T(8,128)(2,1)S(1)}, u32[]{:S(2)}, u32[]{:S(2)}) collective-permute-start(bf16[4,128,128]{2,1,0:T(8,128)(2,1)S(1)} %copy-done.12), channel_id=1, source_target_pairs={{0,2},{1,3},{2,0},{3,1},{4,6},{5,7},{6,4},{7,5},{8,10},{9,11},{10,... | collective-permute-start | bytes 393224 | tf_op jit(solution)/shard_map/ppermute | solution.py:208
  184.5 14.5 %collective-permute-start.10 = (bf16[4,128,128]{2,1,0:T(8,128)(2,1)S(1)}, bf16[4,128,128]{2,1,0:T(8,128)(2,1)S(1)}, u32[]{:S(2)}, u32[]{:S(2)}) collective-permute-start(bf16[4,128,128]{2,1,0:T(8,128)(2,1)S(1)} %copy-done.11), channel_id=1, source_target_pairs={{0,4},{1,5},{2,6},{3,7},{4,0},{5,1},{6,2},{7,3},{8,12},{9,13},{10,... | collective-permute-start | bytes 393224 | tf_op jit(solution)/shard_map/ppermute | solution.py:208
  187.3 17.4 %collective-permute-start.12 = (bf16[4,128,128]{2,1,0:T(8,128)(2,1)S(1)}, bf16[4,128,128]{2,1,0:T(8,128)(2,1)S(1)}, u32[]{:S(2)}, u32[]{:S(2)}) collective-permute-start(bf16[4,128,128]{2,1,0:T(8,128)(2,1)S(1)} %copy-done.10), channel_id=1, source_target_pairs={{0,6},{1,7},{2,4},{3,5},{4,2},{5,3},{6,0},{7,1},{8,14},{9,15},{10,... | collective-permute-start | bytes 393224 | tf_op jit(solution)/shard_map/ppermute | solution.py:208
  188.4 51.9 %copy-start.1 = (bf16[1024,1024]{1,0:T(8,128)(2,1)S(1)}, bf16[1024,1024]{1,0:T(8,128)(2,1)}, u32[]{:S(2)}) copy-start(bf16[1024,1024]{1,0:T(8,128)(2,1)} %refs_21_.1) | copy-start | bytes 6291460
  188.4 51.9 %copy-start.2 = (bf16[1024,1024]{1,0:T(8,128)(2,1)S(1)}, bf16[1024,1024]{1,0:T(8,128)(2,1)}, u32[]{:S(2)}) copy-start(bf16[1024,1024]{1,0:T(8,128)(2,1)} %refs_19_.1) | copy-start | bytes 6291460
  188.4 51.9 %copy-start.3 = (bf16[1024,1024]{1,0:T(8,128)(2,1)S(1)}, bf16[1024,1024]{1,0:T(8,128)(2,1)}, u32[]{:S(2)}) copy-start(bf16[1024,1024]{1,0:T(8,128)(2,1)} %refs_17_.1) | copy-start | bytes 6291460
  197.2 24.3 %collective-permute-start = (bf16[4,128,128]{2,1,0:T(8,128)(2,1)S(1)}, bf16[4,128,128]{2,1,0:T(8,128)(2,1)S(1)}, u32[]{:S(2)}, u32[]{:S(2)}) collective-permute-start(bf16[4,128,128]{2,1,0:T(8,128)(2,1)S(1)} %get-tuple-element.20), channel_id=1, source_target_pairs={{0,1},{1,0},{2,3},{3,2},{4,5},{5,4},{6,7},{7,6},{8,9},{9,8},{10,11... | collective-permute-start | bytes 393224 | tf_op jit(solution)/shard_map/ppermute | solution.py:203
  198.7 27.0 %collective-permute-start.1 = (bf16[4,128,128]{2,1,0:T(8,128)(2,1)S(1)}, bf16[4,128,128]{2,1,0:T(8,128)(2,1)S(1)}, u32[]{:S(2)}, u32[]{:S(2)}) collective-permute-start(bf16[4,128,128]{2,1,0:T(8,128)(2,1)S(1)} %get-tuple-element.21), channel_id=1, source_target_pairs={{0,2},{1,3},{2,0},{3,1},{4,6},{5,7},{6,4},{7,5},{8,10},{9,11},{10,... | collective-permute-start | bytes 393224 | tf_op jit(solution)/shard_map/ppermute | solution.py:203
  199.0 28.1 %collective-permute-start.2 = (bf16[4,128,128]{2,1,0:T(8,128)(2,1)S(1)}, bf16[4,128,128]{2,1,0:T(8,128)(2,1)S(1)}, u32[]{:S(2)}, u32[]{:S(2)}) collective-permute-start(bf16[4,128,128]{2,1,0:T(8,128)(2,1)S(1)} %get-tuple-element.22), channel_id=1, source_target_pairs={{0,3},{1,2},{2,1},{3,0},{4,7},{5,6},{6,5},{7,4},{8,11},{9,10},{10,... | collective-permute-start | bytes 393224 | tf_op jit(solution)/shard_map/ppermute | solution.py:203
  204.7 22.9 %collective-permute-start.3 = (bf16[4,128,128]{2,1,0:T(8,128)(2,1)S(1)}, bf16[4,128,128]{2,1,0:T(8,128)(2,1)S(1)}, u32[]{:S(2)}, u32[]{:S(2)}) collective-permute-start(bf16[4,128,128]{2,1,0:T(8,128)(2,1)S(1)} %get-tuple-element.23), channel_id=1, source_target_pairs={{0,4},{1,5},{2,6},{3,7},{4,0},{5,1},{6,2},{7,3},{8,12},{9,13},{10,... | collective-permute-start | bytes 393224 | tf_op jit(solution)/shard_map/ppermute | solution.py:203
  213.7 18.4 %collective-permute-start.4 = (bf16[4,128,128]{2,1,0:T(8,128)(2,1)S(1)}, bf16[4,128,128]{2,1,0:T(8,128)(2,1)S(1)}, u32[]{:S(2)}, u32[]{:S(2)}) collective-permute-start(bf16[4,128,128]{2,1,0:T(8,128)(2,1)S(1)} %get-tuple-element.24), channel_id=1, source_target_pairs={{0,5},{1,4},{2,7},{3,6},{4,1},{5,0},{6,3},{7,2},{8,13},{9,12},{10,... | collective-permute-start | bytes 393224 | tf_op jit(solution)/shard_map/ppermute | solution.py:203
  221.5 13.7 %collective-permute-start.5 = (bf16[4,128,128]{2,1,0:T(8,128)(2,1)S(1)}, bf16[4,128,128]{2,1,0:T(8,128)(2,1)S(1)}, u32[]{:S(2)}, u32[]{:S(2)}) collective-permute-start(bf16[4,128,128]{2,1,0:T(8,128)(2,1)S(1)} %get-tuple-element.25), channel_id=1, source_target_pairs={{0,6},{1,7},{2,4},{3,5},{4,2},{5,3},{6,0},{7,1},{8,14},{9,15},{10,... | collective-permute-start | bytes 393224 | tf_op jit(solution)/shard_map/ppermute | solution.py:203
  225.7 12.1 %collective-permute-start.6 = (bf16[4,128,128]{2,1,0:T(8,128)(2,1)S(1)}, bf16[4,128,128]{2,1,0:T(8,128)(2,1)S(1)}, u32[]{:S(2)}, u32[]{:S(2)}) collective-permute-start(bf16[4,128,128]{2,1,0:T(8,128)(2,1)S(1)} %get-tuple-element.26), channel_id=1, source_target_pairs={{0,7},{1,6},{2,5},{3,4},{4,3},{5,2},{6,1},{7,0},{8,15},{9,14},{10,... | collective-permute-start | bytes 393224 | tf_op jit(solution)/shard_map/ppermute | solution.py:203
  227.1 10.7 %collective-permute-start.9 = (bf16[4,128,128]{2,1,0:T(8,128)(2,1)S(1)}, bf16[4,128,128]{2,1,0:T(8,128)(2,1)S(1)}, u32[]{:S(2)}, u32[]{:S(2)}) collective-permute-start(bf16[4,128,128]{2,1,0:T(8,128)(2,1)S(1)} %get-tuple-element.34), channel_id=1, source_target_pairs={{0,2},{1,3},{2,0},{3,1},{4,6},{5,7},{6,4},{7,5},{8,10},{9,11},{10,... | collective-permute-start | bytes 393224 | tf_op jit(solution)/shard_map/ppermute | solution.py:208
  227.6 10.5 %collective-permute-start.11 = (bf16[4,128,128]{2,1,0:T(8,128)(2,1)S(1)}, bf16[4,128,128]{2,1,0:T(8,128)(2,1)S(1)}, u32[]{:S(2)}, u32[]{:S(2)}) collective-permute-start(bf16[4,128,128]{2,1,0:T(8,128)(2,1)S(1)} %get-tuple-element.33), channel_id=1, source_target_pairs={{0,4},{1,5},{2,6},{3,7},{4,0},{5,1},{6,2},{7,3},{8,12},{9,13},{10,... | collective-permute-start | bytes 393224 | tf_op jit(solution)/shard_map/ppermute | solution.py:208
  232.1 8.2 %collective-permute-start.13 = (bf16[4,128,128]{2,1,0:T(8,128)(2,1)S(1)}, bf16[4,128,128]{2,1,0:T(8,128)(2,1)S(1)}, u32[]{:S(2)}, u32[]{:S(2)}) collective-permute-start(bf16[4,128,128]{2,1,0:T(8,128)(2,1)S(1)} %get-tuple-element.32), channel_id=1, source_target_pairs={{0,6},{1,7},{2,4},{3,5},{4,2},{5,3},{6,0},{7,1},{8,14},{9,15},{10,... | collective-permute-start | bytes 393224 | tf_op jit(solution)/shard_map/ppermute | solution.py:208
  (4 other events, 126.3 us)

commit v4 on v2

--- a/solution.py
+++ b/solution.py
@@ -13,13 +13,12 @@
     row_tiles, side, cols = feats.shape
     slots = send_ids.shape[0]
 
-    def body(ids, src, out, sem):
-        def issue(i, _):
-            pltpu.make_async_copy(src.at[ids[i]], out.at[i], sem).start()
+    def body(ids, src, out):
+        def step(i, _):
+            out[i] = src[ids[i]]
             return 0
 
-        lax.fori_loop(0, slots, issue, 0, unroll=8)
-        pltpu.make_async_copy(out, out, sem).wait()
+        lax.fori_loop(0, slots, step, 0, unroll=8)
 
     return pl.pallas_call(
         body,
@@ -27,8 +26,7 @@
             num_scalar_prefetch=1,
             grid=(1,),
             in_specs=[pl.BlockSpec((row_tiles, side, cols), lambda i, ids: (0, 0, 0))],
-            out_specs=pl.BlockSpec(memory_space=pl.ANY),
-            scratch_shapes=[pltpu.SemaphoreType.DMA],
+            out_specs=pl.BlockSpec((slots, side, cols), lambda i, ids: (0, 0, 0)),
         ),
         out_shape=jax.ShapeDtypeStruct((slots, side, cols), feats.dtype),
         compiler_params=pltpu.CompilerParams(vmem_limit_bytes=56 << 20),

time: 152 us -> 152 us (level)
  no operation moved by 1% of the time
where the time goes in v4:
time: 152 us
  waiting for transfers between devices  79.9 us (53%)
  starting transfers between devices  45.4 us (30%)
  Pallas kernels  19.9 us (13%)
  matrix products  4.64 us (3%)
    all_to_all x1, waiting for transfers between devices, per_device(): lax.all_to_all(outgoing, 'dom', split_axis=0, concat_axis=0, tiled=True)  64 us
    ppermute x7, starting transfers between devices, exchange(): lax.ppermute(pieces[k], 'section', [(s, s ^ k) for s in range(groups)])  22.3 us
    ppermute x7, starting transfers between devices, swap(): return lax.ppermute(piece, 'section', [(s, s ^ k) for s in range(groups)])  14 us
    ppermute x7, waiting for transfers between devices, swap(): return lax.ppermute(piece, 'section', [(s, s ^ k) for s in range(groups)])  9.22 us
    all_to_all x1, starting transfers between devices, per_device(): lax.all_to_all(outgoing, 'dom', split_axis=0, concat_axis=0, tiled=True)  9.13 us
    pallas_call x1, Pallas kernels, aggregate(): pl.pallas_call(body, grid_spec=pltpu.PrefetchScalarGridSpec(num_scalar_pr...  8.7 us
    ppermute x7, waiting for transfers between devices, exchange(): lax.ppermute(pieces[k], 'section', [(s, s ^ k) for s in range(groups)])  6.73 us
    pallas_call x1, Pallas kernels, finish(): pl.pallas_call(body, grid_spec=pltpu.PrefetchScalarGridSpec(num_scalar_pr...  5.02 us
  transfers between devices with their start and end apart: 15, of which 9 were waited for; matrix products, arithmetic and copies ran while one was open for 3% of the time, Pallas kernels for 7%

profile of v4, /device:TPU:24, one launch (start us, length us, event | category | flops | bytes accessed | tf_op | source)
XLA Modules:
  0.0 152.2 jit_solution(17399865357279187234)
XLA Ops:
  0.6 4.0 %pack_tiles.1 = bf16[96,128,128]{2,1,0:T(8,128)(2,1)} custom-call(s32[96]{0:T(128)} %bitcast.57, bf16[32,128,128]{2,1,0:T(8,128)(2,1)} %bitcast.55), custom_call_target="tpu_custom_call" | custom-call | tf_op jit(solution)/shard_map/pack_tiles/pallas_call | solution.py:23
  4.6 9.1 %all-to-all-start = ((bf16[96,128,128]{2,1,0:T(8,128)(2,1)}), bf16[96,128,128]{2,1,0:T(8,128)(2,1)}, u32[]{:S(2)}, u32[]{:S(2)}) async-start(bf16[96,128,128]{2,1,0:T(8,128)(2,1)} %pack_tiles.1), calls=%async_computation | async-start | bytes 6291456 | tf_op jit(solution)/shard_map/all_to_all | solution.py:232
  13.8 2.2 %own_pieces.1 = (bf16[4,4,128,128]{3,2,1,0:T(8,128)(2,1)}, bf16[4,128,128]{2,1,0:T(8,128)(2,1)}, bf16[4,128,128]{2,1,0:T(8,128)(2,1)}, bf16[4,128,128]{2,1,0:T(8,128)(2,1)}, bf16[4,128,128]{2,1,0:T(8,128)(2,1)}) custom-call(s32[1]{0:T(128)} %bitcast.me_ref, bf16[32,128,128]{2,1,0:T(8,128)(2,1)} %bitcast.56), custom_call_target="tpu_custom_call" | custom-call | tf_op jit(solution)/shard_map/own_pieces/pallas_call | solution.py:49
  16.1 4.6 %add_tanh_fusion.refs_16_ = f32[512,1024]{1,0:T(8,128)S(1)} fusion(bf16[1024,1024]{1,0:T(8,128)(2,1)} %refs_21_.1, f32[1024]{0:T(1024)S(1)} %copy-done.5, bf16[512,1024]{1,0:T(8,128)(2,1)S(1)} %copy-done, bf16[1024,1024]{1,0:T(8,128)(2,1)} %refs_19_.1, f32[1024]{0:T(1024)S(1)} %copy-done.6), kind=kOutput, calls=%fused_computation | convolution fusion | flops 2149056512 | bytes 7348224 | tf_op jit(solution)/shard_map/dot_general | solution.py:236
  20.7 64.0 %all-to-all-done.recv_hbm = bf16[96,128,128]{2,1,0:T(8,128)(2,1)} async-done(((bf16[96,128,128]{2,1,0:T(8,128)(2,1)}), bf16[96,128,128]{2,1,0:T(8,128)(2,1)}, u32[]{:S(2)}, u32[]{:S(2)}) %all-to-all-start) | async-done | bytes 3145760 | tf_op jit(solution)/shard_map/all_to_all | solution.py:232
  84.7 0.7 slice_add_fusion._
  85.4 4.5 %collective-permute-start.7 = (bf16[4,4,128,128]{3,2,1,0:T(8,128)(2,1)}, bf16[4,4,128,128]{3,2,1,0:T(8,128)(2,1)S(1)}, u32[]{:S(2)}, u32[]{:S(2)}) collective-permute-start(bf16[4,4,128,128]{3,2,1,0:T(8,128)(2,1)} %get-tuple-element.28), channel_id=1, source_target_pairs={{0,1},{1,0},{2,3},{3,2},{4,5},{5,4},{6,7},{7,6},{8,9},{9,8},{10,11... | collective-permute-start | bytes 1572872 | tf_op jit(solution)/shard_map/ppermute | solution.py:206
  89.9 1.5 collective-permute-start.8
  91.4 2.7 %collective-permute-start.10 = (bf16[4,128,128]{2,1,0:T(8,128)(2,1)S(1)}, bf16[4,128,128]{2,1,0:T(8,128)(2,1)S(1)}, u32[]{:S(2)}, u32[]{:S(2)}) collective-permute-start(bf16[4,128,128]{2,1,0:T(8,128)(2,1)S(1)} %copy-done.11), channel_id=1, source_target_pairs={{0,4},{1,5},{2,6},{3,7},{4,0},{5,1},{6,2},{7,3},{8,12},{9,13},{10,... | collective-permute-start | bytes 393224 | tf_op jit(solution)/shard_map/ppermute | solution.py:206
  95.3 8.7 %aggregate.1 = (bf16[4,128,128]{2,1,0:T(8,128)(2,1)S(1)}, bf16[4,128,128]{2,1,0:T(8,128)(2,1)S(1)}, bf16[4,128,128]{2,1,0:T(8,128)(2,1)S(1)}, bf16[4,128,128]{2,...) custom-call(s32[256]{0:T(256)S(1)} %copy-done.8, ...), custom_call_target="tpu_custom_call" | custom-call | flops 4294967296 | bytes 12582912 | tf_op jit(solution)/shard_map/aggregate/pallas_call | solution.py:120
  104.0 1.5 %collective-permute-start = (bf16[4,128,128]{2,1,0:T(8,128)(2,1)S(1)}, bf16[4,128,128]{2,1,0:T(8,128)(2,1)S(1)}, u32[]{:S(2)}, u32[]{:S(2)}) collective-permute-start(bf16[4,128,128]{2,1,0:T(8,128)(2,1)S(1)} %get-tuple-element.20), channel_id=1, source_target_pairs={{0,1},{1,0},{2,3},{3,2},{4,5},{5,4},{6,7},{7,6},{8,9},{9,8},{10,11... | collective-permute-start | bytes 393224 | tf_op jit(solution)/shard_map/ppermute | solution.py:201
  105.9 5.7 %collective-permute-start.2 = (bf16[4,128,128]{2,1,0:T(8,128)(2,1)S(1)}, bf16[4,128,128]{2,1,0:T(8,128)(2,1)S(1)}, u32[]{:S(2)}, u32[]{:S(2)}) collective-permute-start(bf16[4,128,128]{2,1,0:T(8,128)(2,1)S(1)} %get-tuple-element.22), channel_id=1, source_target_pairs={{0,3},{1,2},{2,1},{3,0},{4,7},{5,6},{6,5},{7,4},{8,11},{9,10},{10,... | collective-permute-start | bytes 393224 | tf_op jit(solution)/shard_map/ppermute | solution.py:201
  111.5 2.3 %collective-permute-start.3 = (bf16[4,128,128]{2,1,0:T(8,128)(2,1)S(1)}, bf16[4,128,128]{2,1,0:T(8,128)(2,1)S(1)}, u32[]{:S(2)}, u32[]{:S(2)}) collective-permute-start(bf16[4,128,128]{2,1,0:T(8,128)(2,1)S(1)} %get-tuple-element.23), channel_id=1, source_target_pairs={{0,4},{1,5},{2,6},{3,7},{4,0},{5,1},{6,2},{7,3},{8,12},{9,13},{10,... | collective-permute-start | bytes 393224 | tf_op jit(solution)/shard_map/ppermute | solution.py:201
  113.8 6.7 %collective-permute-done.7 = bf16[4,4,128,128]{3,2,1,0:T(8,128)(2,1)S(1)} collective-permute-done((bf16[4,4,128,128]{3,2,1,0:T(8,128)(2,1)}, bf16[4,4,128,128]{3,2,1,0:T(8,128)(2,1)S(1)}, u32[]{:S(2)}, u32[]{:S(2)}) %collective-permute-start.7) | collective-permute-done | bytes 524320 | tf_op jit(solution)/shard_map/ppermute | solution.py:206
  120.5 7.2 %collective-permute-start.4 = (bf16[4,128,128]{2,1,0:T(8,128)(2,1)S(1)}, bf16[4,128,128]{2,1,0:T(8,128)(2,1)S(1)}, u32[]{:S(2)}, u32[]{:S(2)}) collective-permute-start(bf16[4,128,128]{2,1,0:T(8,128)(2,1)S(1)} %get-tuple-element.24), channel_id=1, source_target_pairs={{0,5},{1,4},{2,7},{3,6},{4,1},{5,0},{6,3},{7,2},{8,13},{9,12},{10,... | collective-permute-start | bytes 393224 | tf_op jit(solution)/shard_map/ppermute | solution.py:201
  127.8 0.6 collective-permute-done
  128.4 4.2 %collective-permute-start.5 = (bf16[4,128,128]{2,1,0:T(8,128)(2,1)S(1)}, bf16[4,128,128]{2,1,0:T(8,128)(2,1)S(1)}, u32[]{:S(2)}, u32[]{:S(2)}) collective-permute-start(bf16[4,128,128]{2,1,0:T(8,128)(2,1)S(1)} %get-tuple-element.25), channel_id=1, source_target_pairs={{0,6},{1,7},{2,4},{3,5},{4,2},{5,3},{6,0},{7,1},{8,14},{9,15},{10,... | collective-permute-start | bytes 393224 | tf_op jit(solution)/shard_map/ppermute | solution.py:201
  132.6 1.1 collective-permute-start.6
  134.5 4.0 %collective-permute-start.11 = (bf16[4,128,128]{2,1,0:T(8,128)(2,1)S(1)}, bf16[4,128,128]{2,1,0:T(8,128)(2,1)S(1)}, u32[]{:S(2)}, u32[]{:S(2)}) collective-permute-start(bf16[4,128,128]{2,1,0:T(8,128)(2,1)S(1)} %get-tuple-element.33), channel_id=1, source_target_pairs={{0,4},{1,5},{2,6},{3,7},{4,0},{5,1},{6,2},{7,3},{8,12},{9,13},{10,... | collective-permute-start | bytes 393224 | tf_op jit(solution)/shard_map/ppermute | solution.py:206
  138.4 0.5 collective-permute-done.4
  139.3 2.8 %collective-permute-done.5 = bf16[4,128,128]{2,1,0:T(8,128)(2,1)S(1)} collective-permute-done((bf16[4,128,128]{2,1,0:T(8,128)(2,1)S(1)}, bf16[4,128,128]{2,1,0:T(8,128)(2,1)S(1)}, u32[]{:S(2)}, u32[]{:S(2)}) %collective-permute-start.5) | collective-permute-done | bytes 131104 | tf_op jit(solution)/shard_map/ppermute | solution.py:201
  142.1 2.6 %collective-permute-done.6 = bf16[4,128,128]{2,1,0:T(8,128)(2,1)S(1)} collective-permute-done((bf16[4,128,128]{2,1,0:T(8,128)(2,1)S(1)}, bf16[4,128,128]{2,1,0:T(8,128)(2,1)S(1)}, u32[]{:S(2)}, u32[]{:S(2)}) %collective-permute-start.6) | collective-permute-done | bytes 131104 | tf_op jit(solution)/shard_map/ppermute | solution.py:201
  145.0 2.1 %collective-permute-done.13 = bf16[4,128,128]{2,1,0:T(8,128)(2,1)S(1)} collective-permute-done((bf16[4,128,128]{2,1,0:T(8,128)(2,1)S(1)}, bf16[4,128,128]{2,1,0:T(8,128)(2,1)S(1)}, u32[]{:S(2)}, u32[]{:S(2)}) %collective-permute-start.13) | collective-permute-done | bytes 131104 | tf_op jit(solution)/shard_map/ppermute | solution.py:206
  147.2 5.0 %finish.1 = (bf16[512,1024]{1,0:T(8,128)(2,1)}, bf16[512,1024]{1,0:T(8,128)(2,1)}) custom-call(s32[1]{0:T(128)} %bitcast.me_ref, bf16[512,128]{1,0:T(8,128)(2,1)S(1)} %bitcast.54, bf16[512,128]{1,0:T(8,128)(2,1)S(1)} %bitcast.41, bf16[512,128]{1,0:T(8,128)(2,1)S(1)} %bitcast.42, bf16[512,128]{1,0:T(8,128)(2,1)S(1)} %bitcast.43, ...), custom_call_target="tpu_custom_call" | custom-call | flops 3221225472 | bytes 12582912 | tf_op jit(solution)/shard_map/finish/pallas_call | solution.py:177
  (39 shorter events, 2.3 us)
Async XLA Ops:
  4.6 80.1 %all-to-all-start = ((bf16[96,128,128]{2,1,0:T(8,128)(2,1)}), bf16[96,128,128]{2,1,0:T(8,128)(2,1)}, u32[]{:S(2)}, u32[]{:S(2)}) async-start(bf16[96,128,128]{2,1,0:T(8,128)(2,1)} %pack_tiles.1), calls=%async_computation | async-start | bytes 6291456 | tf_op jit(solution)/shard_map/all_to_all | solution.py:232
  16.0 73.9 %copy-start.12 = (bf16[4,128,128]{2,1,0:T(8,128)(2,1)S(1)}, bf16[4,128,128]{2,1,0:T(8,128)(2,1)}, u32[]{:S(2)}) copy-start(bf16[4,128,128]{2,1,0:T(8,128)(2,1)} %get-tuple-element.29) | copy-start | bytes 393220
  16.0 75.4 %copy-start.11 = (bf16[4,128,128]{2,1,0:T(8,128)(2,1)S(1)}, bf16[4,128,128]{2,1,0:T(8,128)(2,1)}, u32[]{:S(2)}) copy-start(bf16[4,128,128]{2,1,0:T(8,128)(2,1)} %get-tuple-element.30) | copy-start | bytes 393220
  16.0 78.1 %copy-start.10 = (bf16[4,128,128]{2,1,0:T(8,128)(2,1)S(1)}, bf16[4,128,128]{2,1,0:T(8,128)(2,1)}, u32[]{:S(2)}) copy-start(bf16[4,128,128]{2,1,0:T(8,128)(2,1)} %get-tuple-element.31) | copy-start | bytes 393220
  16.0 79.2 %copy-start.8 = (s32[256]{0:T(256)S(1)}, s32[256]{0:T(256)}, u32[]{:S(2)}) copy-start(s32[256]{0:T(256)} %slot_ref.1) | copy-start | bytes 3076
  16.0 79.2 %copy-start.9 = (s32[256]{0:T(256)S(1)}, s32[256]{0:T(256)}, u32[]{:S(2)}) copy-start(s32[256]{0:T(256)} %dst_ref.1) | copy-start | bytes 3076
  85.4 35.2 %collective-permute-start.7 = (bf16[4,4,128,128]{3,2,1,0:T(8,128)(2,1)}, bf16[4,4,128,128]{3,2,1,0:T(8,128)(2,1)S(1)}, u32[]{:S(2)}, u32[]{:S(2)}) collective-permute-start(bf16[4,4,128,128]{3,2,1,0:T(8,128)(2,1)} %get-tuple-element.28), channel_id=1, source_target_pairs={{0,1},{1,0},{2,3},{3,2},{4,5},{5,4},{6,7},{7,6},{8,9},{9,8},{10,11... | collective-permute-start | bytes 1572872 | tf_op jit(solution)/shard_map/ppermute | solution.py:206
  89.9 15.7 %collective-permute-start.8 = (bf16[4,128,128]{2,1,0:T(8,128)(2,1)S(1)}, bf16[4,128,128]{2,1,0:T(8,128)(2,1)S(1)}, u32[]{:S(2)}, u32[]{:S(2)}) collective-permute-start(bf16[4,128,128]{2,1,0:T(8,128)(2,1)S(1)} %copy-done.12), channel_id=1, source_target_pairs={{0,2},{1,3},{2,0},{3,1},{4,6},{5,7},{6,4},{7,5},{8,10},{9,11},{10,... | collective-permute-start | bytes 393224 | tf_op jit(solution)/shard_map/ppermute | solution.py:206
  91.4 14.5 %collective-permute-start.10 = (bf16[4,128,128]{2,1,0:T(8,128)(2,1)S(1)}, bf16[4,128,128]{2,1,0:T(8,128)(2,1)S(1)}, u32[]{:S(2)}, u32[]{:S(2)}) collective-permute-start(bf16[4,128,128]{2,1,0:T(8,128)(2,1)S(1)} %copy-done.11), channel_id=1, source_target_pairs={{0,4},{1,5},{2,6},{3,7},{4,0},{5,1},{6,2},{7,3},{8,12},{9,13},{10,... | collective-permute-start | bytes 393224 | tf_op jit(solution)/shard_map/ppermute | solution.py:206
  94.1 17.4 %collective-permute-start.12 = (bf16[4,128,128]{2,1,0:T(8,128)(2,1)S(1)}, bf16[4,128,128]{2,1,0:T(8,128)(2,1)S(1)}, u32[]{:S(2)}, u32[]{:S(2)}) collective-permute-start(bf16[4,128,128]{2,1,0:T(8,128)(2,1)S(1)} %copy-done.10), channel_id=1, source_target_pairs={{0,6},{1,7},{2,4},{3,5},{4,2},{5,3},{6,0},{7,1},{8,14},{9,15},{10,... | collective-permute-start | bytes 393224 | tf_op jit(solution)/shard_map/ppermute | solution.py:206
  95.3 51.9 %copy-start.1 = (bf16[1024,1024]{1,0:T(8,128)(2,1)S(1)}, bf16[1024,1024]{1,0:T(8,128)(2,1)}, u32[]{:S(2)}) copy-start(bf16[1024,1024]{1,0:T(8,128)(2,1)} %refs_21_.1) | copy-start | bytes 6291460
  95.3 51.9 %copy-start.2 = (bf16[1024,1024]{1,0:T(8,128)(2,1)S(1)}, bf16[1024,1024]{1,0:T(8,128)(2,1)}, u32[]{:S(2)}) copy-start(bf16[1024,1024]{1,0:T(8,128)(2,1)} %refs_19_.1) | copy-start | bytes 6291460
  95.3 51.9 %copy-start.3 = (bf16[1024,1024]{1,0:T(8,128)(2,1)S(1)}, bf16[1024,1024]{1,0:T(8,128)(2,1)}, u32[]{:S(2)}) copy-start(bf16[1024,1024]{1,0:T(8,128)(2,1)} %refs_17_.1) | copy-start | bytes 6291460
  95.3 51.8 %copy-start.4 = (bf16[4,128,128]{2,1,0:T(8,128)(2,1)S(1)}, bf16[4,128,128]{2,1,0:T(8,128)(2,1)}, u32[]{:S(2)}) copy-start(bf16[4,128,128]{2,1,0:T(8,128)(2,1)} %get-tuple-element.27) | copy-start | bytes 393220
  104.0 24.4 %collective-permute-start = (bf16[4,128,128]{2,1,0:T(8,128)(2,1)S(1)}, bf16[4,128,128]{2,1,0:T(8,128)(2,1)S(1)}, u32[]{:S(2)}, u32[]{:S(2)}) collective-permute-start(bf16[4,128,128]{2,1,0:T(8,128)(2,1)S(1)} %get-tuple-element.20), channel_id=1, source_target_pairs={{0,1},{1,0},{2,3},{3,2},{4,5},{5,4},{6,7},{7,6},{8,9},{9,8},{10,11... | collective-permute-start | bytes 393224 | tf_op jit(solution)/shard_map/ppermute | solution.py:201
  105.6 27.0 %collective-permute-start.1 = (bf16[4,128,128]{2,1,0:T(8,128)(2,1)S(1)}, bf16[4,128,128]{2,1,0:T(8,128)(2,1)S(1)}, u32[]{:S(2)}, u32[]{:S(2)}) collective-permute-start(bf16[4,128,128]{2,1,0:T(8,128)(2,1)S(1)} %get-tuple-element.21), channel_id=1, source_target_pairs={{0,2},{1,3},{2,0},{3,1},{4,6},{5,7},{6,4},{7,5},{8,10},{9,11},{10,... | collective-permute-start | bytes 393224 | tf_op jit(solution)/shard_map/ppermute | solution.py:201
  105.9 28.1 %collective-permute-start.2 = (bf16[4,128,128]{2,1,0:T(8,128)(2,1)S(1)}, bf16[4,128,128]{2,1,0:T(8,128)(2,1)S(1)}, u32[]{:S(2)}, u32[]{:S(2)}) collective-permute-start(bf16[4,128,128]{2,1,0:T(8,128)(2,1)S(1)} %get-tuple-element.22), channel_id=1, source_target_pairs={{0,3},{1,2},{2,1},{3,0},{4,7},{5,6},{6,5},{7,4},{8,11},{9,10},{10,... | collective-permute-start | bytes 393224 | tf_op jit(solution)/shard_map/ppermute | solution.py:201
  111.5 23.0 %collective-permute-start.3 = (bf16[4,128,128]{2,1,0:T(8,128)(2,1)S(1)}, bf16[4,128,128]{2,1,0:T(8,128)(2,1)S(1)}, u32[]{:S(2)}, u32[]{:S(2)}) collective-permute-start(bf16[4,128,128]{2,1,0:T(8,128)(2,1)S(1)} %get-tuple-element.23), channel_id=1, source_target_pairs={{0,4},{1,5},{2,6},{3,7},{4,0},{5,1},{6,2},{7,3},{8,12},{9,13},{10,... | collective-permute-start | bytes 393224 | tf_op jit(solution)/shard_map/ppermute | solution.py:201
  120.5 18.4 %collective-permute-start.4 = (bf16[4,128,128]{2,1,0:T(8,128)(2,1)S(1)}, bf16[4,128,128]{2,1,0:T(8,128)(2,1)S(1)}, u32[]{:S(2)}, u32[]{:S(2)}) collective-permute-start(bf16[4,128,128]{2,1,0:T(8,128)(2,1)S(1)} %get-tuple-element.24), channel_id=1, source_target_pairs={{0,5},{1,4},{2,7},{3,6},{4,1},{5,0},{6,3},{7,2},{8,13},{9,12},{10,... | collective-permute-start | bytes 393224 | tf_op jit(solution)/shard_map/ppermute | solution.py:201
  128.4 13.7 %collective-permute-start.5 = (bf16[4,128,128]{2,1,0:T(8,128)(2,1)S(1)}, bf16[4,128,128]{2,1,0:T(8,128)(2,1)S(1)}, u32[]{:S(2)}, u32[]{:S(2)}) collective-permute-start(bf16[4,128,128]{2,1,0:T(8,128)(2,1)S(1)} %get-tuple-element.25), channel_id=1, source_target_pairs={{0,6},{1,7},{2,4},{3,5},{4,2},{5,3},{6,0},{7,1},{8,14},{9,15},{10,... | collective-permute-start | bytes 393224 | tf_op jit(solution)/shard_map/ppermute | solution.py:201
  132.6 12.1 %collective-permute-start.6 = (bf16[4,128,128]{2,1,0:T(8,128)(2,1)S(1)}, bf16[4,128,128]{2,1,0:T(8,128)(2,1)S(1)}, u32[]{:S(2)}, u32[]{:S(2)}) collective-permute-start(bf16[4,128,128]{2,1,0:T(8,128)(2,1)S(1)} %get-tuple-element.26), channel_id=1, source_target_pairs={{0,7},{1,6},{2,5},{3,4},{4,3},{5,2},{6,1},{7,0},{8,15},{9,14},{10,... | collective-permute-start | bytes 393224 | tf_op jit(solution)/shard_map/ppermute | solution.py:201
  134.0 10.7 %collective-permute-start.9 = (bf16[4,128,128]{2,1,0:T(8,128)(2,1)S(1)}, bf16[4,128,128]{2,1,0:T(8,128)(2,1)S(1)}, u32[]{:S(2)}, u32[]{:S(2)}) collective-permute-start(bf16[4,128,128]{2,1,0:T(8,128)(2,1)S(1)} %get-tuple-element.34), channel_id=1, source_target_pairs={{0,2},{1,3},{2,0},{3,1},{4,6},{5,7},{6,4},{7,5},{8,10},{9,11},{10,... | collective-permute-start | bytes 393224 | tf_op jit(solution)/shard_map/ppermute | solution.py:206
  134.5 10.5 %collective-permute-start.11 = (bf16[4,128,128]{2,1,0:T(8,128)(2,1)S(1)}, bf16[4,128,128]{2,1,0:T(8,128)(2,1)S(1)}, u32[]{:S(2)}, u32[]{:S(2)}) collective-permute-start(bf16[4,128,128]{2,1,0:T(8,128)(2,1)S(1)} %get-tuple-element.33), channel_id=1, source_target_pairs={{0,4},{1,5},{2,6},{3,7},{4,0},{5,1},{6,2},{7,3},{8,12},{9,13},{10,... | collective-permute-start | bytes 393224 | tf_op jit(solution)/shard_map/ppermute | solution.py:206
  138.9 8.2 %collective-permute-start.13 = (bf16[4,128,128]{2,1,0:T(8,128)(2,1)S(1)}, bf16[4,128,128]{2,1,0:T(8,128)(2,1)S(1)}, u32[]{:S(2)}, u32[]{:S(2)}) collective-permute-start(bf16[4,128,128]{2,1,0:T(8,128)(2,1)S(1)} %get-tuple-element.32), channel_id=1, source_target_pairs={{0,6},{1,7},{2,4},{3,5},{4,2},{5,3},{6,0},{7,1},{8,14},{9,15},{10,... | collective-permute-start | bytes 393224 | tf_op jit(solution)/shard_map/ppermute | solution.py:206
  (4 other events, 90.0 us)
